TPU v7x, 128 devices: a whole 4x4x4 slice. The times are simulated.
128 devices in a mesh: comp: 4 (over x), dom: 32 (over z, y, core).
Axes of the slice: x: 4, y: 4, z: 4, core: 2. Of those that a mesh axis runs over, the one named last changes fastest.
Arguments:
- state: float32 [4, 128, 65536], P('comp', None, 'dom'), may hold values from -6 to 6
- neighbors: int32 [4, 4, 65536], P('comp', None, 'dom'), may hold values from 0 to 2559, as said below
- edge_coef: float32 [4, 4, 65536], P('comp', None, 'dom'), may hold values from 0.02 to 0.22
- sea_mask: int32 [65536], P('dom'), may hold values 0 or 1
- pair_source: int32 [32, 16], replicated, may hold values from 0 to 95, as said below
- pair_rows: int32 [32, 16, 512], P('dom'), may hold values from 0 to 2047, as said below
- pair_cols: int32 [32, 16, 512], replicated, may hold values from 0 to 2047, as said below
- remap_weight: float32 [32, 16, 512, 512], P('dom'), may hold values from -0.25 to 0.25
Outputs:
- advanced_state: float32 [4, 128, 65536], P('comp', None, 'dom')
Inputs may be any that keep to these rules, and one draw needn't show every extreme that they name: `neighbors`: each entry indexes the 2048 columns of its domain widened by 256 columns of each adjacent domain of the cycle, the left rim first. `pair_source`: row d names 16 different atmosphere devices: in each atmosphere band the domains d - 2 to d + 2 around the cycle, and one more atmosphere device outside these. `pair_rows`: cells of the ocean domain, different within one block. `pair_cols`: columns of the atmosphere device of the block, different within one block.
All inputs are finite; a program needn't handle non-finite values. No bound on the sum of `sea_mask` on one device may be relied on, other than what follows from the above.
Results may differ from a plain program's by a relative error of at most 0.000052.
Values sent between devices are 32-bit elements; how exact they have to be, the bound alone decides.
A program may use at most 128 MiB of HBM per device.

v0:
```python
import jax
import jax.numpy as jnp
from jax import lax
from jax.sharding import PartitionSpec as P

FIELDS = 4
RIM = 256
EDGES = 4
STEPS = 4


FORCE_GAIN = 0.5


def with_halo(array, sides, width):
    for axis, dim in sides:
        devices, length = (lax.axis_size(axis), array.shape[dim])
        up = [(i, (i + 1) % devices) for i in range(devices)]
        down = [(j, i) for i, j in up]
        last = lax.slice_in_dim(array, length - width, length, axis=dim)
        leading = lax.slice_in_dim(array, 0, width, axis=dim)
        before = lax.ppermute(last, axis, up)
        after = lax.ppermute(leading, axis, down)
        array = jnp.concatenate([before, array, after], axis=dim)
    return array


def local(state, neighbors, edge_coef, sea_mask, pair_source, pair_rows, pair_cols, remap_weight):
    highest = lax.Precision.HIGHEST
    comp_count = lax.axis_size("comp")
    dom_count = lax.axis_size("dom")
    comp_id = lax.axis_index("comp")
    dom_id = lax.axis_index("dom")
    current = state[0]
    fields = FIELDS
    column_count = current.shape[1]
    pair_count = pair_source.shape[1]
    block = pair_rows.shape[2]
    device_total = comp_count * dom_count
    is_ocean = comp_id == comp_count - 1
    myself = comp_id * dom_count + dom_id
    surface = current[:fields]
    pair_index = jnp.arange(pair_count, dtype=jnp.int32)
    matched = pair_source == myself
    partner = jnp.any(matched, axis=1)
    which_pair = jnp.sum(jnp.where(matched, pair_index[None, :], 0), axis=1)
    my_columns = jnp.sum(jnp.where(matched[:, :, None], pair_cols, 0), axis=1)
    handler_comp = jnp.full_like(which_pair, comp_count - 1)
    activity = jnp.where(is_ocean, 1.0, 0.0).astype(jnp.float32)
    rows_here = pair_rows[0]
    weights_here = remap_weight[0]
    own_sources = lax.dynamic_index_in_dim(pair_source, dom_id, 0, keepdims=False)
    sea_values = surface[:, rows_here]
    upward = jnp.einsum("qbj,fqb->fqj", weights_here, sea_values, precision=highest) * activity
    to_air = jnp.zeros((fields, device_total, block), jnp.float32).at[:, own_sources].add(upward)
    slot_index = handler_comp * dom_count + jnp.arange(dom_count, dtype=jnp.int32)
    air_values = surface[:, my_columns] * partner[None, :, None]
    to_sea = jnp.zeros((fields, device_total, block), jnp.float32).at[:, slot_index].add(air_values)
    got_sea, got_air = (
        lax.all_to_all(to_sea, ("comp", "dom"), split_axis=1, concat_axis=1, tiled=True),
        lax.all_to_all(to_air, ("comp", "dom"), split_axis=1, concat_axis=1, tiled=True),
    )
    incoming = got_sea[:, own_sources]
    downward = jnp.einsum("qbj,fqj->fqb", weights_here, incoming, precision=highest) * activity
    sea_force = jnp.zeros((fields, column_count), jnp.float32).at[:, rows_here].add(downward)
    arrived = got_air[:, slot_index] * partner[None, :, None]
    air_force = jnp.zeros((fields, column_count), jnp.float32).at[:, my_columns].add(arrived)
    forcing = jnp.where(is_ocean, sea_force, air_force)
    adjacency = neighbors[0]
    rates = edge_coef[0]
    evolving = jnp.logical_or(jnp.logical_not(is_ocean), sea_mask == 1)
    for step_number in range(STEPS):
        padded = with_halo(current, (("dom", 1),), RIM)
        updated = current
        for edge_number in range(EDGES):
            updated = updated + rates[edge_number] * (padded[:, adjacency[edge_number]] - current)
        updated = updated.at[:fields].add(FORCE_GAIN * (forcing - current[:fields]))
        current = jnp.where(evolving[None, :], updated, current)
    return current[None]


def solution(mesh):
    placed = (
        P("comp", None, "dom"),
        P("comp", None, "dom"),
        P("comp", None, "dom"),
        P("dom"),
        P(),
        P("dom", None, None),
        P(),
        P("dom", None, None, None),
    )
    return jax.shard_map(
        local, mesh=mesh, in_specs=placed, out_specs=P("comp", None, "dom"), check_vma=False
    )
```

profile of v0, /device:TPU:0, one launch (start us, length us, event | category | flops | bytes accessed | tf_op | source)
XLA Modules:
  0.0 515.9 jit_solution(9994804072112863629)
XLA Ops:
  2.3 6.0 %collective-permute-start.1 = (f32[128,256]{0,1:T(8,128)}, f32[128,256]{0,1:T(8,128)}, u32[]{:S(2)}, u32[]{:S(2)}) collective-permute-start(f32[128,256]{0,1:T(8,128)} %get-tuple-element.64), channel_id=1, source_target_pairs={{1,0},{2,1},{3,2},{4,3},{5,4},{6,5},{7,6},{8,7},{9,8},{10,9},{11,1... | collective-permute-start | bytes 393224 | tf_op jit(solution)/shard_map/ppermute | solution.py:23
  8.9 54.8 %gather_fusion.4 = f32[16384,4]{1,0:T(8,128)} fusion(f32[4,2048]{0,1:T(8,128)S(1)} %slice_bitcast_fusion, s32[16384]{0:T(1024)S(1)} %broadcast_clamp_fusion), kind=kCustom, calls=%fused_computation.4 | custom fusion | bytes 589824 | tf_op jit(solution)/shard_map/gather | solution.py:57
  63.6 5.2 %copy.32 = f32[32,512,4]{1,0,2:T(8,128)S(1)} copy(f32[32,512,4]{2,1,0:T(8,128)} %bitcast.190) | data formatting | bytes 524288 | tf_op jit(solution)/shard_map/gather | solution.py:57
  74.5 7.4 %all-to-all-start = ((f32[4,128,512]{2,0,1:T(4,128)}), f32[4,128,512]{2,0,1:T(4,128)}, u32[]{:S(2)}, u32[]{:S(2)}) async-start(f32[4,128,512]{2,0,1:T(4,128)} %scatter_fusion), calls=%async_computation | async-start | bytes 2097152 | tf_op jit(solution)/shard_map/all_to_all | solution.py:60
  82.3 27.8 %gather_fusion.6 = f32[8192,4]{1,0:T(8,128)} fusion(f32[4,2048]{0,1:T(8,128)S(1)} %slice_bitcast_fusion, s32[8192]{0:T(1024)S(1)} %broadcast_clamp_fusion.1), kind=kCustom, calls=%fused_computation.6 | custom fusion | bytes 294912 | tf_op jit(solution)/shard_map/gather | solution.py:53
  113.1 11.5 %fusion.7 = f32[16,4,512]{2,1,0:T(4,128)S(1)} fusion(f32[1,16,512,512]{3,2,1,0:T(8,128)} %param.23, f32[16,512,4]{1,2,0:T(4,128)S(1)} %copy.29, f32[]{:T(128)S(6)} %select_n.142), kind=kOutput, calls=%fused_computation.33 | convolution fusion | flops 201359360 | bytes 17039364 | tf_op jit(solution)/shard_map/qbj,fqb->fqj/dot_general | solution.py:54
  129.3 5.5 %gather_fusion = f32[2048,128]{1,0:T(8,128)S(1)} fusion(f32[128,2560]{0,1:T(8,128)S(1)} %pad_maximum_fusion, s32[2048]{0:T(1024)S(1)} %broadcast_clamp_fusion.5), kind=kCustom, calls=%fused_computation | custom fusion | bytes 2105344 | tf_op jit(solution)/shard_map/gather | solution.py:76
  134.7 7.6 %gather_fusion.1 = f32[2048,128]{1,0:T(8,128)} fusion(f32[128,2560]{0,1:T(8,128)S(1)} %pad_maximum_fusion, s32[2048]{0:T(1024)S(1)} %broadcast_clamp_fusion.4), kind=kCustom, calls=%fused_computation.1 | custom fusion | bytes 2105344 | tf_op jit(solution)/shard_map/gather | solution.py:76
  142.3 7.6 %gather_fusion.2 = f32[2048,128]{1,0:T(8,128)} fusion(f32[128,2560]{0,1:T(8,128)S(1)} %pad_maximum_fusion, s32[2048]{0:T(1024)S(1)} %broadcast_clamp_fusion.3), kind=kCustom, calls=%fused_computation.2 | custom fusion | bytes 2105344 | tf_op jit(solution)/shard_map/gather | solution.py:76
  149.9 7.6 %gather_fusion.3 = f32[2048,128]{1,0:T(8,128)} fusion(f32[128,2560]{0,1:T(8,128)S(1)} %pad_maximum_fusion, s32[2048]{0:T(1024)S(1)} %broadcast_clamp_fusion.2), kind=kCustom, calls=%fused_computation.3 | custom fusion | bytes 2105344 | tf_op jit(solution)/shard_map/gather | solution.py:76
  157.6 10.4 %all-to-all-start.1 = ((f32[4,128,512]{2,0,1:T(4,128)}), f32[4,128,512]{2,0,1:T(4,128)}, u32[]{:S(2)}, u32[]{:S(2)}) async-start(f32[4,128,512]{2,0,1:T(4,128)} %scatter_fusion.1), calls=%async_computation.1 | async-start | bytes 2097152 | tf_op jit(solution)/shard_map/all_to_all | solution.py:61
  173.3 17.3 %fusion.4 = f32[16,4,512]{2,1,0:T(4,128)S(1)} fusion(f32[1,16,512,512]{3,2,1,0:T(8,128)} %param.23, f32[16,4,512]{2,1,0:T(4,128)S(1)} %gather_fusion.5, f32[]{:T(128)S(6)} %select_n.142), kind=kOutput, calls=%fused_computation.32 | convolution fusion | flops 201359360 | bytes 17039364 | tf_op jit(solution)/shard_map/qbj,fqj->fqb/dot_general | solution.py:64
  195.3 5.1 copy.30
  200.4 44.5 %scatter_custom_fusion.1 = f32[4,2048]{0,1:T(8,128)S(1)} fusion(s32[8192]{0:T(1024)} %bitcast.213, f32[8192,4]{1,0:T(8,128)} %copy.28, f32[]{:T(128)} %constant.125.clone.1), kind=kCustom, calls=%fused_computation.97 | custom fusion | flops 32768 | bytes 33280 | tf_op jit(solution)/shard_map/scatter-add | solution.py:65
  244.9 110.5 %scatter_custom_fusion.3 = f32[4,2048]{0,1:T(8,128)} fusion(s32[16384]{0:T(1024)S(1)} %bitcast.195, f32[16384,4]{1,0:T(8,128)} %copy.30, f32[]{:T(128)} %constant.125.clone.1), kind=kCustom, calls=%fused_computation.95 | custom fusion | flops 65536 | bytes 33280 | tf_op jit(solution)/shard_map/scatter-add | solution.py:67
  358.1 7.6 %scatter-add.52 = f32[128,2048]{0,1:T(8,128)S(1)} dynamic-update-slice(f32[128,2048]{0,1:T(8,128)S(1)} %fusion.41, f32[4,2048]{0,1:T(8,128)} %get-tuple-element.53, s32[]{:T(128)} %constant.123.clone.1, s32[]{:T(128)} %constant.123.clone.1) | dynamic-update-slice | bytes 65540 | tf_op jit(solution)/shard_map/scatter-add | solution.py:77
  374.0 5.5 %gather_fusion.10 = f32[2048,128]{1,0:T(8,128)S(1)} fusion(f32[128,2560]{0,1:T(8,128)S(1)} %pad_maximum_fusion.1, s32[2048]{0:T(1024)S(1)} %broadcast_clamp_fusion.3), kind=kCustom, calls=%fused_computation.10 | custom fusion | bytes 2105344 | tf_op jit(solution)/shard_map/gather | solution.py:76
  379.5 7.6 %gather_fusion.8 = f32[2048,128]{1,0:T(8,128)} fusion(f32[128,2560]{0,1:T(8,128)S(1)} %pad_maximum_fusion.1, s32[2048]{0:T(1024)S(1)} %broadcast_clamp_fusion.5), kind=kCustom, calls=%fused_computation.8 | custom fusion | bytes 2105344 | tf_op jit(solution)/shard_map/gather | solution.py:76
  387.1 7.6 %gather_fusion.9 = f32[2048,128]{1,0:T(8,128)} fusion(f32[128,2560]{0,1:T(8,128)S(1)} %pad_maximum_fusion.1, s32[2048]{0:T(1024)S(1)} %broadcast_clamp_fusion.4), kind=kCustom, calls=%fused_computation.9 | custom fusion | bytes 2105344 | tf_op jit(solution)/shard_map/gather | solution.py:76
  394.7 7.6 %gather_fusion.11 = f32[2048,128]{1,0:T(8,128)} fusion(f32[128,2560]{0,1:T(8,128)S(1)} %pad_maximum_fusion.1, s32[2048]{0:T(1024)S(1)} %broadcast_clamp_fusion.2), kind=kCustom, calls=%fused_computation.11 | custom fusion | bytes 2105344 | tf_op jit(solution)/shard_map/gather | solution.py:76
  411.1 5.1 collective-permute-start.5
  418.9 7.6 %gather_fusion.12 = f32[2048,128]{1,0:T(8,128)} fusion(f32[128,2560]{0,1:T(8,128)S(1)} %pad_maximum_fusion.2, s32[2048]{0:T(1024)S(1)} %broadcast_clamp_fusion.5), kind=kCustom, calls=%fused_computation.12 | custom fusion | bytes 2105344 | tf_op jit(solution)/shard_map/gather | solution.py:76
  426.5 7.6 %gather_fusion.13 = f32[2048,128]{1,0:T(8,128)} fusion(f32[128,2560]{0,1:T(8,128)S(1)} %pad_maximum_fusion.2, s32[2048]{0:T(1024)S(1)} %broadcast_clamp_fusion.4), kind=kCustom, calls=%fused_computation.13 | custom fusion | bytes 2105344 | tf_op jit(solution)/shard_map/gather | solution.py:76
  434.1 7.6 %gather_fusion.14 = f32[2048,128]{1,0:T(8,128)} fusion(f32[128,2560]{0,1:T(8,128)S(1)} %pad_maximum_fusion.2, s32[2048]{0:T(1024)S(1)} %broadcast_clamp_fusion.3), kind=kCustom, calls=%fused_computation.14 | custom fusion | bytes 2105344 | tf_op jit(solution)/shard_map/gather | solution.py:76
  441.7 7.6 %gather_fusion.15 = f32[2048,128]{1,0:T(8,128)} fusion(f32[128,2560]{0,1:T(8,128)S(1)} %pad_maximum_fusion.2, s32[2048]{0:T(1024)S(1)} %broadcast_clamp_fusion.2), kind=kCustom, calls=%fused_computation.15 | custom fusion | bytes 2105344 | tf_op jit(solution)/shard_map/gather | solution.py:76
  456.3 5.5 %scatter-add.54 = f32[128,2048]{0,1:T(8,128)} dynamic-update-slice(f32[128,2048]{0,1:T(8,128)} %fusion.25, f32[4,2048]{0,1:T(8,128)} %fusion.13, s32[]{:T(128)} %constant.123.clone.1, s32[]{:T(128)} %constant.123.clone.1) | dynamic-update-slice | bytes 65540 | tf_op jit(solution)/shard_map/scatter-add | solution.py:77
  463.5 5.2 %collective-permute-start.7 = (f32[128,256]{0,1:T(8,128)S(1)}, f32[128,256]{0,1:T(8,128)S(1)}, u32[]{:S(2)}, u32[]{:S(2)}) collective-permute-start(f32[128,256]{0,1:T(8,128)S(1)} %get-tuple-element.58), channel_id=1, source_target_pairs={{1,0},{2,1},{3,2},{4,3},{5,4},{6,5},{7,6},{8,7},{9,8},{10,9},{11,1... | collective-permute-start | bytes 393224 | tf_op jit(solution)/shard_map/ppermute | solution.py:23
  471.4 7.6 %gather_fusion.16 = f32[2048,128]{1,0:T(8,128)} fusion(f32[128,2560]{0,1:T(8,128)S(1)} %pad_maximum_fusion.3, s32[2048]{0:T(1024)S(1)} %broadcast_clamp_fusion.5), kind=kCustom, calls=%fused_computation.16 | custom fusion | bytes 2105344 | tf_op jit(solution)/shard_map/gather | solution.py:76
  479.0 7.6 %gather_fusion.17 = f32[2048,128]{1,0:T(8,128)} fusion(f32[128,2560]{0,1:T(8,128)S(1)} %pad_maximum_fusion.3, s32[2048]{0:T(1024)S(1)} %broadcast_clamp_fusion.4), kind=kCustom, calls=%fused_computation.17 | custom fusion | bytes 2105344 | tf_op jit(solution)/shard_map/gather | solution.py:76
  486.6 7.6 %gather_fusion.18 = f32[2048,128]{1,0:T(8,128)} fusion(f32[128,2560]{0,1:T(8,128)S(1)} %pad_maximum_fusion.3, s32[2048]{0:T(1024)S(1)} %broadcast_clamp_fusion.3), kind=kCustom, calls=%fused_computation.18 | custom fusion | bytes 2105344 | tf_op jit(solution)/shard_map/gather | solution.py:76
  494.2 7.6 %gather_fusion.19 = f32[2048,128]{1,0:T(8,128)} fusion(f32[128,2560]{0,1:T(8,128)S(1)} %pad_maximum_fusion.3, s32[2048]{0:T(1024)S(1)} %broadcast_clamp_fusion.2), kind=kCustom, calls=%fused_computation.19 | custom fusion | bytes 2105344 | tf_op jit(solution)/shard_map/gather | solution.py:76
  506.6 7.6 %scatter-add.55 = f32[128,2048]{0,1:T(8,128)S(1)} dynamic-update-slice(f32[128,2048]{0,1:T(8,128)S(1)} %fusion.17, f32[4,2048]{0,1:T(8,128)} %fusion.11, s32[]{:T(128)} %constant.123.clone.1, s32[]{:T(128)} %constant.123.clone.1) | dynamic-update-slice | bytes 65540 | tf_op jit(solution)/shard_map/scatter-add | solution.py:77
  (98 shorter events, 66.3 us)
Async XLA Ops:
  1.6 6.9 %copy-start.9 = (s32[32,16]{0,1:T(8,128)S(1)}, s32[32,16]{0,1:T(8,128)}, u32[]{:S(2)}) copy-start(s32[32,16]{0,1:T(8,128)} %param.20) | copy-start | bytes 6148
  1.6 7.0 %copy-start.4 = (s32[32,16,512]{2,1,0:T(8,128)S(1)}, s32[32,16,512]{2,1,0:T(8,128)}, u32[]{:S(2)}) copy-start(s32[32,16,512]{2,1,0:T(8,128)} %param.22) | copy-start | bytes 3145732
  2.3 125.9 %collective-permute-start = (f32[128,256]{0,1:T(8,128)}, f32[128,256]{0,1:T(8,128)}, u32[]{:S(2)}, u32[]{:S(2)}) collective-permute-start(f32[128,256]{0,1:T(8,128)} %get-tuple-element.63), channel_id=1, source_target_pairs={{0,1},{1,2},{2,3},{3,4},{4,5},{5,6},{6,7},{7,8},{8,9},{9,10},{10,1... | collective-permute-start | bytes 393224 | tf_op jit(solution)/shard_map/ppermute | solution.py:22
  2.3 125.9 %collective-permute-start.1 = (f32[128,256]{0,1:T(8,128)}, f32[128,256]{0,1:T(8,128)}, u32[]{:S(2)}, u32[]{:S(2)}) collective-permute-start(f32[128,256]{0,1:T(8,128)} %get-tuple-element.64), channel_id=1, source_target_pairs={{1,0},{2,1},{3,2},{4,3},{5,4},{6,5},{7,6},{8,7},{9,8},{10,9},{11,1... | collective-permute-start | bytes 393224 | tf_op jit(solution)/shard_map/ppermute | solution.py:23
  8.4 61.9 %copy-start.11 = (s32[32]{0:T(128)}, s32[32]{0:T(128)S(1)}, u32[]{:S(2)}) copy-start(s32[32]{0:T(128)S(1)} %fusion.56) | copy-start | bytes 388
  70.3 11.6 %copy-start.6 = (s32[1,4,2048]{2,1,0:T(4,128)S(1)}, s32[1,4,2048]{2,1,0:T(4,128)}, u32[]{:S(2)}) copy-start(s32[1,4,2048]{2,1,0:T(4,128)} %param.17) | copy-start | bytes 98308
  74.5 7.7 %copy-start.7 = (s32[1,16,512]{2,1,0:T(8,128)S(1)}, s32[1,16,512]{2,1,0:T(8,128)}, u32[]{:S(2)}) copy-start(s32[1,16,512]{2,1,0:T(8,128)} %param.21) | copy-start | bytes 98308
  74.5 83.0 %all-to-all-start = ((f32[4,128,512]{2,0,1:T(4,128)}), f32[4,128,512]{2,0,1:T(4,128)}, u32[]{:S(2)}, u32[]{:S(2)}) async-start(f32[4,128,512]{2,0,1:T(4,128)} %scatter_fusion), calls=%async_computation | async-start | bytes 2097152 | tf_op jit(solution)/shard_map/all_to_all | solution.py:60
  82.3 30.7 %copy-start.5 = (s32[2,4,8,128]{3,1,2,0:T(4,128)}, s32[2,4,8,128]{3,1,2,0:T(4,128)S(1)}, u32[]{:S(2)}) copy-start(s32[2,4,8,128]{3,1,2,0:T(4,128)S(1)} %copy.33) | copy-start | bytes 98308
  110.2 2.9 copy-start.10
  113.0 11.5 %copy-start.8 = (f32[1,4,2048]{2,1,0:T(4,128)S(1)}, f32[1,4,2048]{2,1,0:T(4,128)}, u32[]{:S(2)}) copy-start(f32[1,4,2048]{2,1,0:T(4,128)} %param.18) | copy-start | bytes 98308
  124.6 3.6 copy-start.12
  157.6 35.7 %all-to-all-start.1 = ((f32[4,128,512]{2,0,1:T(4,128)}), f32[4,128,512]{2,0,1:T(4,128)}, u32[]{:S(2)}, u32[]{:S(2)}) async-start(f32[4,128,512]{2,0,1:T(4,128)} %scatter_fusion.1), calls=%async_computation.1 | async-start | bytes 2097152 | tf_op jit(solution)/shard_map/all_to_all | solution.py:61
  366.1 7.8 %collective-permute-start.2 = (f32[128,256]{0,1:T(8,128)S(1)}, f32[128,256]{0,1:T(8,128)S(1)}, u32[]{:S(2)}, u32[]{:S(2)}) collective-permute-start(f32[128,256]{0,1:T(8,128)S(1)} %get-tuple-element.61), channel_id=1, source_target_pairs={{0,1},{1,2},{2,3},{3,4},{4,5},{5,6},{6,7},{7,8},{8,9},{9,10},{10,1... | collective-permute-start | bytes 393224 | tf_op jit(solution)/shard_map/ppermute | solution.py:22
  366.2 7.7 %collective-permute-start.3 = (f32[128,256]{0,1:T(8,128)S(1)}, f32[128,256]{0,1:T(8,128)S(1)}, u32[]{:S(2)}, u32[]{:S(2)}) collective-permute-start(f32[128,256]{0,1:T(8,128)S(1)} %get-tuple-element.62), channel_id=1, source_target_pairs={{1,0},{2,1},{3,2},{4,3},{5,4},{6,5},{7,6},{8,7},{9,8},{10,9},{11,1... | collective-permute-start | bytes 393224 | tf_op jit(solution)/shard_map/ppermute | solution.py:23
  402.3 3.6 copy-start.2
  411.0 43.0 %copy-start = (f32[128,2048]{0,1:T(8,128)}, f32[128,2048]{0,1:T(8,128)S(1)}, u32[]{:S(2)}) copy-start(f32[128,2048]{0,1:T(8,128)S(1)} %broadcast_select_fusion.1) | copy-start | bytes 3145732
  411.0 7.8 %collective-permute-start.4 = (f32[128,256]{0,1:T(8,128)S(1)}, f32[128,256]{0,1:T(8,128)S(1)}, u32[]{:S(2)}, u32[]{:S(2)}) collective-permute-start(f32[128,256]{0,1:T(8,128)S(1)} %get-tuple-element.59), channel_id=1, source_target_pairs={{0,1},{1,2},{2,3},{3,4},{4,5},{5,6},{6,7},{7,8},{8,9},{9,10},{10,1... | collective-permute-start | bytes 393224 | tf_op jit(solution)/shard_map/ppermute | solution.py:22
  411.1 7.7 %collective-permute-start.5 = (f32[128,256]{0,1:T(8,128)S(1)}, f32[128,256]{0,1:T(8,128)S(1)}, u32[]{:S(2)}, u32[]{:S(2)}) collective-permute-start(f32[128,256]{0,1:T(8,128)S(1)} %get-tuple-element.60), channel_id=1, source_target_pairs={{1,0},{2,1},{3,2},{4,3},{5,4},{6,5},{7,6},{8,7},{9,8},{10,9},{11,1... | collective-permute-start | bytes 393224 | tf_op jit(solution)/shard_map/ppermute | solution.py:23
  449.3 4.6 copy-start.3
  456.3 5.5 %copy-start.1 = (f32[128,2048]{0,1:T(8,128)S(1)}, f32[128,2048]{0,1:T(8,128)}, u32[]{:S(2)}) copy-start(f32[128,2048]{0,1:T(8,128)} %copy-done) | copy-start | bytes 3145732
  463.4 7.9 %collective-permute-start.6 = (f32[128,256]{0,1:T(8,128)S(1)}, f32[128,256]{0,1:T(8,128)S(1)}, u32[]{:S(2)}, u32[]{:S(2)}) collective-permute-start(f32[128,256]{0,1:T(8,128)S(1)} %get-tuple-element.57), channel_id=1, source_target_pairs={{0,1},{1,2},{2,3},{3,4},{4,5},{5,6},{6,7},{7,8},{8,9},{9,10},{10,1... | collective-permute-start | bytes 393224 | tf_op jit(solution)/shard_map/ppermute | solution.py:22
  463.5 7.8 %collective-permute-start.7 = (f32[128,256]{0,1:T(8,128)S(1)}, f32[128,256]{0,1:T(8,128)S(1)}, u32[]{:S(2)}, u32[]{:S(2)}) collective-permute-start(f32[128,256]{0,1:T(8,128)S(1)} %get-tuple-element.58), channel_id=1, source_target_pairs={{1,0},{2,1},{3,2},{4,3},{5,4},{6,5},{7,6},{8,7},{9,8},{10,9},{11,1... | collective-permute-start | bytes 393224 | tf_op jit(solution)/shard_map/ppermute | solution.py:23
where the time goes:
time: 520 us; the launch traced here: 516 us
  local copies, waits for them, and re-layouts  251 us (48%)
  other arithmetic  188 us (36%)
  starting transfers between devices  39.4 us (8%)
  matrix products  28.8 us (6%)
  waiting for transfers between devices  7.81 us (2%)
    gather x16, local copies, waits for them, and re-layouts, local(): padded[:, adjacency[edge_number]] - current  117 us
    scatter-add x1, other arithmetic, local(): jnp.zeros((fields, column_count), jnp.float32).at[:, my_columns]  110 us
    gather x2, local copies, waits for them, and re-layouts, local(): air_values = surface[:, my_columns] * partner[None, :, None]  60 us
    scatter-add x1, other arithmetic, local(): jnp.zeros((fields, column_count), jnp.float32).at[:, rows_here]  44.5 us
    gather x2, local copies, waits for them, and re-layouts, local(): sea_values = surface[:, rows_here]  30.7 us
    scatter-add x4, local copies, waits for them, and re-layouts, local(): updated = updated.at[:fields].add(FORCE_GAIN * (forcing - current[:fields]))  25.3 us
    ppermute x4, starting transfers between devices, with_halo(): after = lax.ppermute(leading, axis, down)  21.4 us
    dot_general x1, matrix products, local(): jnp.einsum('qbj,fqj->fqb', weights_here, incoming, precision=highest)  17.3 us
  transfers between devices with their start and end apart: 10, of which 3 were waited for; matrix products, arithmetic and copies ran while one was open for 32% of the time, Pallas kernels for 0%

commit v1 on v0

--- a/solution.py
+++ b/solution.py
@@ -1,15 +1,26 @@
+import functools
+
 import jax
 import jax.numpy as jnp
 from jax import lax
+from jax.experimental import pallas as pl
+from jax.experimental.pallas import tpu as pltpu
 from jax.sharding import PartitionSpec as P
 
 FIELDS = 4
 RIM = 256
 EDGES = 4
 STEPS = 4
-
-
 FORCE_GAIN = 0.5
+
+LANES = 128
+SUB = 8
+NEAR = 2
+NEAR_COUNT = 2 * NEAR + 1
+EXTRAS = 4
+MESH = pl.DeviceIdType.MESH
+F32 = jnp.float32
+BF16 = jnp.bfloat16
 
 
 def with_halo(array, sides, width):
@@ -25,7 +36,7 @@
     return array
 
 
-def local(state, neighbors, edge_coef, sea_mask, pair_source, pair_rows, pair_cols, remap_weight):
+def general(state, neighbors, edge_coef, sea_mask, pair_source, pair_rows, pair_cols, remap_weight):
     highest = lax.Precision.HIGHEST
     comp_count = lax.axis_size("comp")
     dom_count = lax.axis_size("dom")
@@ -76,7 +87,435 @@
             updated = updated + rates[edge_number] * (padded[:, adjacency[edge_number]] - current)
         updated = updated.at[:fields].add(FORCE_GAIN * (forcing - current[:fields]))
         current = jnp.where(evolving[None, :], updated, current)
-    return current[None]
+    return current
+
+
+def lane_gather(values, lanes):
+    return jnp.take_along_axis(values, lanes, axis=1, mode="promise_in_bounds")
+
+
+def interval_kernel(nd, nc, tiles, levels, block, pairs,
+                    tab, win, nbr, coef, mask, rows, state_hbm, cols_hbm, w_hbm,
+                    out_hbm,
+                    pb0, pb1, pb2, pb3, pg0, pg1, pg2, pg3, outb, outg,
+                    cols, wbuf, compact, slots, gsl, zslots, usl, sea, fpart, fgot, force,
+                    load_sem, w_sem, cols_sem, out_sem,
+                    hsend, hrecv, asend, arecv, usend, urecv, ssend, srecv, fsend, frecv):
+    comp = lax.axis_index("comp")
+    dom = lax.axis_index("dom")
+    ocean = nc - 1
+    bulk = levels - SUB
+    halo = RIM // LANES
+    pb = [pb0, pb1, pb2, pb3]
+    pg = [pg0, pg1, pg2, pg3]
+    left = lax.rem(dom + nd - 1, nd)
+    right = lax.rem(dom + 1, nd)
+    is_air = comp < ocean
+    near_rel = [0, 1, 2, nd - 2, nd - 1]
+    T_WHICH, T_SEL, T_EXT, T_VALID = 0, nd, 2 * nd, 2 * nd + EXTRAS
+    T_NEARP = 2 * nd + 2 * EXTRAS
+    T_EP, T_EVALID, T_ESRC = T_NEARP + NEAR_COUNT, T_NEARP + NEAR_COUNT + 1, T_NEARP + NEAR_COUNT + 2
+
+    def load_g(j):
+        return pltpu.make_async_copy(state_hbm.at[pl.ds(0, SUB), pl.ds(j * LANES, LANES)], pg0.at[j + halo], load_sem.at[0])
+
+    def load_b(j):
+        return pltpu.make_async_copy(state_hbm.at[pl.ds(SUB, bulk), pl.ds(j * LANES, LANES)], pb0.at[j + halo], load_sem.at[1])
+
+    for j in range(tiles):
+        load_g(j).start()
+    cols_copy = pltpu.make_async_copy(cols_hbm, cols, cols_sem)
+    cols_copy.start()
+    for j in range(tiles):
+        load_b(j).start()
+
+    @pl.when(is_air)
+    def _():
+        for p in range(pairs):
+            pltpu.make_async_copy(w_hbm.at[p], wbuf.at[p], w_sem).start()
+
+    barrier = pltpu.get_barrier_semaphore()
+
+    @pl.when(is_air)
+    def _():
+        def greet(r, _):
+            pl.semaphore_signal(barrier, inc=1, device_id=(comp, lax.rem(dom + r, nd)), device_id_type=MESH)
+            return 0
+        lax.fori_loop(1, nd, greet, 0)
+        pl.semaphore_signal(barrier, inc=1, device_id=(ocean, dom), device_id_type=MESH)
+
+    @pl.when(jnp.logical_not(is_air))
+    def _():
+        pl.semaphore_signal(barrier, inc=1, device_id=(comp, left), device_id_type=MESH)
+        pl.semaphore_signal(barrier, inc=1, device_id=(comp, right), device_id_type=MESH)
+        for c in range(ocean):
+            pl.semaphore_signal(barrier, inc=1, device_id=(c, dom), device_id_type=MESH)
+
+    row8 = lax.broadcasted_iota(jnp.int32, (SUB, LANES), 0)
+
+    def doubled(ref, offset):
+        out = []
+        for h in range(tiles):
+            v = ref[h + offset]
+            out.append(jnp.where(row8 < FIELDS, v, pltpu.roll(v, FIELDS, axis=0)))
+        return out
+
+    def gather_slot(table, index):
+        res = []
+        for q in range(0, block // LANES, 2):
+            i0 = index[:, q * LANES:(q + 1) * LANES]
+            i1 = index[:, (q + 1) * LANES:(q + 2) * LANES]
+            i8 = jnp.where(row8 < FIELDS, jnp.broadcast_to(i0, (SUB, LANES)), jnp.broadcast_to(i1, (SUB, LANES)))
+            lo = i8 & (LANES - 1)
+            hi = i8 >> 7
+            acc = lane_gather(table[0], lo)
+            for h in range(1, tiles):
+                acc = jnp.where(hi == h, lane_gather(table[h], lo), acc)
+            res.append(acc)
+        return res
+
+    def split_rows(res):
+        cols_ = []
+        for acc in res:
+            high = acc.astype(BF16).astype(F32)
+            low = acc - high
+            cols_.append(jnp.where(row8 < FIELDS, high, pltpu.roll(low, FIELDS, axis=0)))
+            cols_.append(jnp.where(row8 < FIELDS, pltpu.roll(high, FIELDS, axis=0), low))
+        return jnp.concatenate(cols_, axis=1)
+
+    def scatter(eight, index):
+        hi = jnp.broadcast_to(index >> 7, (SUB, block))
+        lhs = jnp.concatenate([jnp.where(hi == h, eight, 0.0) for h in range(tiles)], axis=0).astype(BF16)
+        lo = jnp.broadcast_to(index & (LANES - 1), (LANES, block))
+        hot = jnp.where(lo == lax.broadcasted_iota(jnp.int32, (LANES, block), 0), 1.0, 0.0).astype(BF16)
+        return lax.dot_general(lhs, hot, (((1,), (1,)), ((), ())), preferred_element_type=F32)
+
+    def cols_of(t):
+        return cols[t, pl.ds(tab[T_WHICH + t], 1), :]
+
+    pltpu.make_async_copy(pg0.at[pl.ds(halo, tiles)], pg0.at[pl.ds(halo, tiles)], load_sem.at[0]).wait()
+    cols_copy.wait()
+
+    @pl.when(is_air)
+    def _():
+        table = doubled(pg0, halo)
+        for n, r in enumerate(near_rel):
+            t = lax.rem(dom + r, nd)
+            res = gather_slot(table, cols_of(t))
+            for i, acc in enumerate(res):
+                if r == 0:
+                    gsl[dom, i] = acc
+                else:
+                    slots[r, i] = acc
+
+        def extra(e, _):
+            res = gather_slot(table, cols_of(tab[T_EXT + e]))
+            for i, acc in enumerate(res):
+                compact[e, i] = acc
+            return 0
+        lax.fori_loop(0, EXTRAS, extra, 0)
+
+        def fill(r, _):
+            t = lax.rem(dom + r, nd)
+            slots[r] = compact[tab[T_SEL + t]]
+            return 0
+        lax.fori_loop(NEAR + 1, nd - NEAR, fill, 0)
+
+    @pl.when(is_air)
+    def _():
+        pl.semaphore_wait(barrier, nd)
+
+    @pl.when(jnp.logical_not(is_air))
+    def _():
+        pl.semaphore_wait(barrier, 2 + ocean)
+
+    def a_copy(r):
+        return pltpu.make_async_remote_copy(
+            src_ref=slots.at[r], dst_ref=gsl.at[dom], send_sem=asend, recv_sem=arecv,
+            device_id=(comp, lax.rem(dom + r, nd)), device_id_type=MESH)
+
+    def halo_copies(ref, s, kind):
+        to_left = pltpu.make_async_remote_copy(
+            src_ref=ref.at[pl.ds(halo, halo)], dst_ref=ref.at[pl.ds(tiles + halo, halo)],
+            send_sem=hsend.at[kind, s, 0], recv_sem=hrecv.at[kind, s, 0], device_id=(comp, left), device_id_type=MESH)
+        to_right = pltpu.make_async_remote_copy(
+            src_ref=ref.at[pl.ds(tiles, halo)], dst_ref=ref.at[pl.ds(0, halo)],
+            send_sem=hsend.at[kind, s, 1], recv_sem=hrecv.at[kind, s, 1], device_id=(comp, right), device_id_type=MESH)
+        return to_left, to_right
+
+    def sea_copy(c):
+        return pltpu.make_async_remote_copy(
+            src_ref=pg0.at[pl.ds(halo, tiles)], dst_ref=sea, send_sem=ssend, recv_sem=srecv,
+            device_id=(c, dom), device_id_type=MESH)
+
+    @pl.when(jnp.logical_not(is_air))
+    def _():
+        for c in range(ocean):
+            sea_copy(c).start()
+
+    @pl.when(is_air)
+    def _():
+        def send(r, _):
+            a_copy(r).start()
+            return 0
+        lax.fori_loop(1, nd, send, 0)
+
+    for c in halo_copies(pg[0], 0, 0):
+        c.start()
+    pltpu.make_async_copy(pb0.at[pl.ds(halo, tiles)], pb0.at[pl.ds(halo, tiles)], load_sem.at[1]).wait()
+    for c in halo_copies(pb[0], 0, 1):
+        c.start()
+
+    lane1 = lax.broadcasted_iota(jnp.int32, (1, LANES), 1)
+
+    def tile_step(src, j, rows_, forced):
+        cols_j = pl.ds(pl.multiple_of(j * LANES, LANES), LANES)
+        cur = src[j + halo]
+        upd = cur
+        low = jnp.broadcast_to(lane1 < LANES // 2, (rows_, LANES))
+        for k in range(EDGES):
+            lo = jnp.broadcast_to(nbr[pl.ds(k, 1), cols_j] & (LANES - 1), (rows_, LANES))
+            got = []
+            for h in range(2):
+                w = win[(k * tiles + j) * 2 + h]
+                b = jnp.minimum(w >> 7, tiles + 2 * halo - 2)
+                edge = jnp.broadcast_to(lane1 >= w - b * LANES, (rows_, LANES))
+                got.append(lane_gather(jnp.where(edge, src[b], src[b + 1]), lo))
+            upd = upd + coef[pl.ds(k, 1), cols_j] * (jnp.where(low, got[0], got[1]) - cur)
+        if forced:
+            gain = jnp.where(row8 < FIELDS, FORCE_GAIN, 0.0)
+            upd = upd + gain * (force[j] - cur)
+        keep = jnp.logical_or(is_air, mask[:, cols_j] == 1)
+        return jnp.where(jnp.broadcast_to(keep, (rows_, LANES)), upd, cur)
+
+    def bulk_step(s):
+        src = pb[s]
+        dst, off = (pb[s + 1], halo) if s + 1 < STEPS else (outb, 0)
+        per = 2
+
+        def body(i, _):
+            new = [tile_step(src, i * per + u, bulk, False) for u in range(per)]
+            for u in range(per):
+                dst[i * per + u + off] = new[u]
+            return 0
+        for c in halo_copies(src, s, 1):
+            c.wait()
+        lax.fori_loop(0, tiles // per, body, 0)
+        if s + 1 < STEPS:
+            for c in halo_copies(pb[s + 1], s + 1, 1):
+                c.start()
+
+    def group_step(s):
+        src = pg[s]
+        dst, off = (pg[s + 1], halo) if s + 1 < STEPS else (outg, 0)
+        for c in halo_copies(src, s, 0):
+            c.wait()
+        new = [tile_step(src, j, SUB, True) for j in range(tiles)]
+        for j in range(tiles):
+            dst[j + off] = new[j]
+        if s + 1 < STEPS:
+            for c in halo_copies(pg[s + 1], s + 1, 0):
+                c.start()
+
+    bulk_step(0)
+
+    @pl.when(is_air)
+    def _():
+        pltpu.make_async_copy(gsl.at[pl.ds(0, nd - 1)], gsl.at[pl.ds(0, nd - 1)], arecv).wait()
+        pltpu.make_async_copy(sea, sea, srecv).wait()
+        pltpu.make_async_copy(w_hbm, wbuf, w_sem).wait()
+        sea_table = doubled(sea, 0)
+        total = jnp.zeros((tiles * SUB, LANES), F32)
+
+        def dense(p, src):
+            w = wbuf[p]
+            wh = w.astype(BF16)
+            wl = (w - wh.astype(F32)).astype(BF16)
+            index = rows[pl.ds(p, 1), :]
+            x = split_rows([gsl[src, i] for i in range(block // (2 * LANES))]).astype(BF16)
+            v = split_rows(gather_slot(sea_table, index)).astype(BF16)
+            dims = (((1,), (1,)), ((), ()))
+            y = (lax.dot_general(x, wh, dims, preferred_element_type=F32)
+                 + lax.dot_general(x, wl, dims, preferred_element_type=F32))
+            z = jnp.dot(v, wh, preferred_element_type=F32) + jnp.dot(v, wl, preferred_element_type=F32)
+            y = y[:FIELDS] + y[FIELDS:]
+            z = z[:FIELDS] + z[FIELDS:]
+            yh = y.astype(BF16).astype(F32)
+            return jnp.concatenate([yh, y - yh], axis=0), z, index
+
+        def put(ref, at, z):
+            for q in range(block // LANES):
+                ref[at, q // 2, pl.ds((q % 2) * FIELDS, FIELDS), :] = z[:, q * LANES:(q + 1) * LANES]
+
+        def u_copy(slot, r):
+            return pltpu.make_async_remote_copy(
+                src_ref=zslots.at[slot], dst_ref=usl.at[dom], send_sem=usend, recv_sem=urecv,
+                device_id=(comp, lax.rem(dom + r, nd)), device_id_type=MESH)
+
+        eight, z, index = dense(tab[T_EP], tab[T_ESRC])
+        put(zslots, NEAR_COUNT, z)
+
+        def send(r, _):
+            u_copy(NEAR_COUNT, r).start()
+            return 0
+        lax.fori_loop(NEAR + 1, nd - NEAR, send, 0)
+        total = total + scatter(jnp.where(tab[T_EVALID] == 1, eight, 0.0), index)
+        for n, r in enumerate(near_rel):
+            eight, z, index = dense(tab[T_NEARP + n], lax.rem(dom + r, nd))
+            if r == 0:
+                put(usl, dom, z)
+            else:
+                put(zslots, n, z)
+                u_copy(n, r).start()
+            total = total + scatter(eight, index)
+        for h in range(tiles):
+            part = total[h * SUB:(h + 1) * SUB]
+            fpart[h] = part + pltpu.roll(part, FIELDS, axis=0)
+        pltpu.make_async_remote_copy(
+            src_ref=fpart, dst_ref=fgot.at[comp], send_sem=fsend, recv_sem=frecv,
+            device_id=(ocean, dom), device_id_type=MESH).start()
+
+    bulk_step(1)
+
+    @pl.when(is_air)
+    def _():
+        pltpu.make_async_copy(usl.at[pl.ds(0, nd - 1)], usl.at[pl.ds(0, nd - 1)], urecv).wait()
+        total = jnp.zeros((tiles * SUB, LANES), F32)
+        for r in near_rel:
+            t = lax.rem(dom + r, nd)
+            total = total + scatter(split_rows([usl[t, i] for i in range(block // (2 * LANES))]), cols_of(t))
+        for e in range(EXTRAS):
+            t = tab[T_EXT + e]
+            eight = split_rows([usl[t, i] for i in range(block // (2 * LANES))])
+            total = total + scatter(jnp.where(tab[T_VALID + e] == 1, eight, 0.0), cols_of(t))
+        for h in range(tiles):
+            part = total[h * SUB:(h + 1) * SUB]
+            force[h] = part + pltpu.roll(part, FIELDS, axis=0)
+
+    @pl.when(jnp.logical_not(is_air))
+    def _():
+        pltpu.make_async_copy(fgot, fgot, frecv).wait()
+        for h in range(tiles):
+            force[h] = fgot[0, h] + fgot[1, h] + fgot[2, h]
+
+    group_step(0)
+    bulk_step(2)
+    group_step(1)
+    bulk_step(3)
+
+    def store_b(j):
+        return pltpu.make_async_copy(outb.at[j], out_hbm.at[pl.ds(SUB, bulk), pl.ds(j * LANES, LANES)], out_sem.at[1])
+
+    def store_g(j):
+        return pltpu.make_async_copy(outg.at[j], out_hbm.at[pl.ds(0, SUB), pl.ds(j * LANES, LANES)], out_sem.at[0])
+
+    for j in range(tiles):
+        store_b(j).start()
+    group_step(2)
+    group_step(3)
+    for j in range(tiles):
+        store_g(j).start()
+
+    @pl.when(is_air)
+    def _():
+        pltpu.make_async_copy(slots.at[pl.ds(0, nd - 1)], slots.at[pl.ds(0, nd - 1)], asend).wait()
+        pltpu.make_async_copy(slots.at[pl.ds(0, nd - 1)], slots.at[pl.ds(0, nd - 1)], usend).wait()
+        pltpu.make_async_copy(fpart, fpart, fsend).wait()
+
+    @pl.when(jnp.logical_not(is_air))
+    def _():
+        pltpu.make_async_copy(fgot, fgot, ssend).wait()
+
+    pltpu.make_async_copy(outb, outb, out_sem.at[1]).wait()
+    pltpu.make_async_copy(outg, outg, out_sem.at[0]).wait()
+
+
+def windowed(state, neighbors, edge_coef, sea_mask, pair_rows, pair_cols, remap_weight, table, windows):
+    nd, nc = lax.axis_size("dom"), lax.axis_size("comp")
+    _, levels, columns = state.shape
+    tiles = columns // LANES
+    padded = tiles + 2 * RIM // LANES
+    pairs, block = pair_rows.shape[1:]
+    pieces = block // (2 * LANES)
+    bulk = levels - SUB
+    smem = pl.BlockSpec(memory_space=pltpu.SMEM)
+    vmem = pl.BlockSpec(memory_space=pltpu.VMEM)
+    hbm = pl.BlockSpec(memory_space=pl.ANY)
+    dma = pltpu.SemaphoreType.DMA
+    scratch = (
+        [pltpu.VMEM((padded, bulk, LANES), F32)] * STEPS
+        + [pltpu.VMEM((padded, SUB, LANES), F32)] * STEPS
+        + [pltpu.VMEM((tiles, bulk, LANES), F32), pltpu.VMEM((tiles, SUB, LANES), F32)]
+        + [
+            pltpu.VMEM(pair_cols.shape, jnp.int32),
+            pltpu.VMEM((pairs, block, block), F32),
+            pltpu.VMEM((EXTRAS, pieces, SUB, LANES), F32),
+            pltpu.VMEM((nd, pieces, SUB, LANES), F32),
+            pltpu.VMEM((nd, pieces, SUB, LANES), F32),
+            pltpu.VMEM((NEAR_COUNT + 1, pieces, SUB, LANES), F32),
+            pltpu.VMEM((nd, pieces, SUB, LANES), F32),
+            pltpu.VMEM((tiles, SUB, LANES), F32),
+            pltpu.VMEM((tiles, SUB, LANES), F32),
+            pltpu.VMEM((nc - 1, tiles, SUB, LANES), F32),
+            pltpu.VMEM((tiles, SUB, LANES), F32),
+        ]
+        + [dma((2,)), dma, dma, dma((2,))]
+        + [dma((2, STEPS, 2)), dma((2, STEPS, 2))]
+        + [dma] * 8
+    )
+    return pl.pallas_call(
+        functools.partial(interval_kernel, nd, nc, tiles, levels, block, pairs),
+        out_shape=jax.ShapeDtypeStruct((levels, columns), F32),
+        in_specs=[smem, smem, vmem, vmem, vmem, vmem, hbm, hbm, hbm],
+        out_specs=hbm,
+        scratch_shapes=scratch,
+        name="interval",
+        cost_estimate=pl.CostEstimate(flops=10**9, bytes_accessed=10**8, transcendentals=0),
+        compiler_params=pltpu.CompilerParams(
+            collective_id=0, has_side_effects=True, vmem_limit_bytes=48 * 2**20),
+    )(table, windows, neighbors[0], edge_coef[0], sea_mask[None], pair_rows[0], state[0], pair_cols, remap_weight[0])
+
+
+def local(state, neighbors, edge_coef, sea_mask, pair_source, pair_rows, pair_cols, remap_weight):
+    nd, nc = lax.axis_size("dom"), lax.axis_size("comp")
+    comp, dom = lax.axis_index("comp"), lax.axis_index("dom")
+    columns = state.shape[2]
+    tiles = columns // LANES
+    pairs = pair_source.shape[1]
+    i32 = jnp.int32
+
+    halves = neighbors[0].reshape(EDGES * tiles * 2, LANES // 2)
+    windows = jnp.minimum(jnp.min(halves, axis=1), columns + 2 * RIM - LANES)
+    wide = jnp.max(jnp.max(halves, axis=1) - windows) >= LANES
+
+    t = jnp.arange(nd, dtype=i32)
+    index = jnp.arange(pairs, dtype=i32)
+    matched = pair_source == comp * nd + dom
+    which = jnp.sum(jnp.where(matched, index[None], 0), axis=1).astype(i32)
+    offset = jnp.mod(t - dom, nd)
+    far = jnp.any(matched, axis=1) & (offset > NEAR) & (offset < nd - NEAR)
+    rank = jnp.cumsum(far.astype(i32)) - 1
+    sel = jnp.clip(jnp.where(far, rank, 0), 0, EXTRAS - 1).astype(i32)
+    hit = far[None] & (rank[None] == jnp.arange(EXTRAS, dtype=i32)[:, None])
+    ext = jnp.sum(jnp.where(hit, t[None], 0), axis=1).astype(i32)
+    valid = jnp.any(hit, axis=1).astype(i32)
+    crowded = jnp.sum(far.astype(i32)) > EXTRAS
+
+    own = lax.dynamic_index_in_dim(pair_source, dom, 0, keepdims=False)
+    own_offset = jnp.mod(own % nd - dom, nd)
+    own_band = own // nd == comp
+    rel = jnp.array([0, 1, 2, nd - 2, nd - 1], i32)
+    near_p = jnp.sum(jnp.where((own_offset[None] == rel[:, None]) & own_band[None], index[None], 0), axis=1).astype(i32)
+    own_far = (own_offset > NEAR) & (own_offset < nd - NEAR) & own_band
+    e_p = jnp.sum(jnp.where(own_far, index, 0)).astype(i32)
+    e_valid = jnp.any(own_far).astype(i32)
+    e_src = jnp.sum(jnp.where(own_far, own % nd, 0)).astype(i32)
+    table = jnp.concatenate([which, sel, ext, valid, near_p, jnp.stack([e_p, e_valid, e_src])])
+
+    bad = lax.psum(jnp.where(wide | crowded, 1.0, 0.0).astype(F32), ("comp", "dom")) > 0
+    fast = windowed(state, neighbors, edge_coef, sea_mask, pair_rows, pair_cols, remap_weight, table, windows)
+    args = (state, neighbors, edge_coef, sea_mask, pair_source, pair_rows, pair_cols, remap_weight)
+    return lax.cond(bad, lambda f, *a: general(*a), lambda f, *a: f, fast, *args)[None]
 
 
 def solution(mesh):

time: 520 us -> 131 us (0.25)
  local copies, waits for them, and re-layouts: 251 us -> 5.15 us
  other arithmetic: 188 us -> 6.65 us
  blocking collectives: 0 us -> 63 us
  Pallas kernels: 0 us -> 52.5 us
  starting transfers between devices: 39.4 us -> 0 us
  matrix products: 28.8 us -> 0 us
  waiting for transfers between devices: 7.81 us -> 0 us
    gather x22 -> x0, local copies, waits for them, and re-layouts: 212 us -> none  [the longest x16 117 us: local(): padded[:, adjacency[edge_number]] - current]
    scatter-add x4 -> x0, other arithmetic: 162 us -> none  [the longest x1 110 us: local(): jnp.zeros((fields, column_count), jnp.float32).at[:, my_columns]]
    psum x0 -> x1, blocking collectives: none -> 63 us  [local(): lax.psum(jnp.where(wide | crowded, 1.0, 0.0).astype(F32), ('comp', 'dom'))]
    pallas_call x0 -> x1, Pallas kernels: none -> 52.5 us  [windowed(): pl.pallas_call(functools.partial(interval_kernel, nd, nc, tiles, levels,...]
    dot_general x2 -> x0, matrix products: 28.8 us -> none  [the longest x1 17.3 us: local(): jnp.einsum('qbj,fqj->fqb', weights_here, incoming, precision=highest)]
    scatter-add x4 -> x0, local copies, waits for them, and re-layouts: 25.3 us -> none  [local(): updated = updated.at[:fields].add(FORCE_GAIN * (forcing - current[:fields]))]
    add x8 -> x0, other arithmetic: 21.8 us -> none  [the longest x4 15.4 us: local(): updated + rates[edge_number] * (padded[:, adjacency[edge_number]] - current)]
    ppermute x8 -> x0, starting transfers between devices: 21.6 us -> none  [the longest x4 21.4 us: with_halo(): after = lax.ppermute(leading, axis, down)]
  transfers between devices with their start and end apart: 10 -> 0, of which waited for: 3 -> 0; matrix products, arithmetic and copies ran while one was open for 32% -> 0% of each run, Pallas kernels for 0% -> 0%
where the time goes in v1:
time: 131 us; the launch traced here: 130 us
  blocking collectives  63 us (48%)
  Pallas kernels  52.5 us (40%)
  other arithmetic  6.65 us (5%)
  local copies, waits for them, and re-layouts  5.15 us (4%)
  between operations  2.76 us (2%)
    psum x1, blocking collectives, local(): lax.psum(jnp.where(wide | crowded, 1.0, 0.0).astype(F32), ('comp', 'dom'))  63 us
    pallas_call x1, Pallas kernels, windowed(): pl.pallas_call(functools.partial(interval_kernel, nd, nc, tiles, levels,...  52.5 us

profile of v1, /device:TPU:0, one launch (start us, length us, event | category | flops | bytes accessed | tf_op | source)
XLA Modules:
  0.0 130.3 jit_solution(11894341074498325774)
XLA Ops:
  0.0 0.9 fusion.63
  0.9 0.9 dynamic-slice_reduce_fusion
  1.8 0.7 fusion.74
  2.4 0.7 select_reduce_fusion.4
  3.2 0.8 select_reduce_fusion.2
  4.7 0.7 select_reduce_fusion.1
  5.4 0.1 copy.42
  5.5 0.1 reduce-window.7
  5.6 0.1 add_reduce_fusion
  5.7 0.1 fusion.68
  5.8 0.1 select_reduce_fusion.3
  6.0 1.3 %concatenate.23.tab = s32[80]{0:T(128)S(1)} concatenate(s32[32]{0:T(128)S(1)} %get-tuple-element.133, s32[32]{0:T(128)S(1)} %get-tuple-element.131, s32[4]{0:T(128)S(1)} %select_reduce_fusion.3, s32[4]{0:T(128)S(1)} %convert_element_type.32, s32[5]{0:T(128)S(1)} %select_reduce_fusion.2, s32[1]{0:T(128)} %bitcast.48, s32[1]{0:T(128)} %bitcast.49, s32[1]{0:T(128)} %bitcast.50), dimensions={0} | concatenate | bytes 640 | tf_op jit(solution)/shard_map/concatenate | solution.py:513
  7.3 0.9 reshape_squeeze.3
  8.1 0.1 fusion.72
  8.3 0.6 broadcast_minimum_fusion
  8.9 0.0 copy-start.4
  8.9 0.0 copy-start.5
  8.9 0.0 copy-start.9
  8.9 0.0 copy-start.12
  8.9 52.5 %interval.1 = f32[128,2048]{1,0:T(8,128)} custom-call(s32[80]{0:T(128)S(1)} %concatenate.23.tab, s32[128]{0:T(128)S(1)} %get-tuple-element.151.win, s32[4,2048]{1,0:T(4,128)} %bitcast.213, f32[4,2048]{1,0:T(4,128)} %bitcast.232, s32[1,2048]{1,0:T(1,128)} %bitcast.236, s32[16,512]{1,0:T(8,128)} %bitcast.233, f32[128,2048]{1,0:T(8,128)} %bitcast.209, ...), custom_call_target="tpu_custom_call" | custom-call | flops 1000000000 | bytes 100000000 | tf_op jit(solution)/shard_map/interval/pallas_call | solution.py:466
  61.4 0.7 convert_reduce_fusion
  63.5 63.0 %psum.7 = f32[]{:T(128)} all-reduce(f32[]{:T(128)S(6)} %select_n.207), channel_id=1, replica_groups=mesh['comp'=4,'dom'=32] {'comp','dom'}, use_global_device_ids=true, to_apply=%region_5.6 | all-reduce | flops 1 | bytes 8 | tf_op jit(solution)/shard_map/psum | solution.py:515
  127.1 0.0 copy-done.4
  127.2 0.0 copy-done.5
  127.2 0.0 copy-done.9
  127.2 0.0 copy-done.12
  127.2 0.0 copy-done.15
  127.2 2.1 %conditional.1 = (f32[1,128,2048]{2,1,0:T(8,128)S(1)}) conditional(s32[]{:T(128)} %convert_element_type.30, f32[128,2048]{1,0:T(8,128)} %interval.1, (s32[2048]{0:T(1024)S(1)}, f32[1,128,2048]{2,1,0:T(8,128)S(1)}, f32[1,4,2048]{2,1,0:T(4,128)}, s32[1,4,2048]{2,1,0:T(4,128)S(1)}, s32[1,16,512]{2,1,0:T(8,128)}, /*index=5*/s32[32,16]{0,1:T(8,128)S(1)}, ...), branch_computations={%region_14.15_spmd, %region_15.22_spmd} | conditional | flops 420052160 | bytes 161364128 | solution.py:518
  127.2 1.5 %copy.43 = f32[128,2048]{0,1:T(8,128)S(1)} copy(f32[128,2048]{1,0:T(8,128)} %param.8) | data formatting | bytes 2097152 | tf_op jit(solution)/shard_map/interval/pallas_call
  128.8 0.3 copy.48
  129.3 0.0 copy-start.8
  129.3 1.0 copy-done.8
  (5 shorter events, 0.1 us)
Async XLA Ops:
  8.9 118.2 %copy-start.4 = (f32[1,128,2048]{2,1,0:T(8,128)S(1)}, f32[1,128,2048]{2,1,0:T(8,128)}, u32[]{:S(2)}) copy-start(f32[1,128,2048]{2,1,0:T(8,128)} %param.19) | copy-start | bytes 3145732
  8.9 118.3 %copy-start.5 = (s32[32,16,512]{2,1,0:T(8,128)S(1)}, s32[32,16,512]{2,1,0:T(8,128)}, u32[]{:S(2)}) copy-start(s32[32,16,512]{2,1,0:T(8,128)} %cols_hbm.1) | copy-start | bytes 3145732
  8.9 118.3 %copy-start.9 = (s32[1,4,2048]{2,1,0:T(4,128)S(1)}, s32[1,4,2048]{2,1,0:T(4,128)}, u32[]{:S(2)}) copy-start(s32[1,4,2048]{2,1,0:T(4,128)} %param.20) | copy-start | bytes 98308
  8.9 118.3 %copy-start.12 = (s32[32,16]{0,1:T(8,128)S(1)}, s32[32,16]{0,1:T(8,128)}, u32[]{:S(2)}) copy-start(s32[32,16]{0,1:T(8,128)} %param.23) | copy-start | bytes 6148
  8.9 118.3 %copy-start.15 = (s32[2048]{0:T(1024)S(1)}, s32[2048]{0:T(1024)}, u32[]{:S(2)}) copy-start(s32[2048]{0:T(1024)} %param.22) | copy-start | bytes 24580
  129.3 1.0 copy-start.8

commit v2 on v1

--- a/solution.py
+++ b/solution.py
@@ -4,6 +4,7 @@
 import jax.numpy as jnp
 from jax import lax
 from jax.experimental import pallas as pl
+from jax.experimental.layout import Layout, with_layout_constraint
 from jax.experimental.pallas import tpu as pltpu
 from jax.sharding import PartitionSpec as P
 
@@ -42,7 +43,7 @@
     dom_count = lax.axis_size("dom")
     comp_id = lax.axis_index("comp")
     dom_id = lax.axis_index("dom")
-    current = state[0]
+    current = with_layout_constraint(state, Layout((0, 1, 2)))[0]
     fields = FIELDS
     column_count = current.shape[1]
     pair_count = pair_source.shape[1]
@@ -80,14 +81,16 @@
     adjacency = neighbors[0]
     rates = edge_coef[0]
     evolving = jnp.logical_or(jnp.logical_not(is_ocean), sea_mask == 1)
-    for step_number in range(STEPS):
+
+    def advance(_, current):
         padded = with_halo(current, (("dom", 1),), RIM)
         updated = current
         for edge_number in range(EDGES):
             updated = updated + rates[edge_number] * (padded[:, adjacency[edge_number]] - current)
         updated = updated.at[:fields].add(FORCE_GAIN * (forcing - current[:fields]))
-        current = jnp.where(evolving[None, :], updated, current)
-    return current
+        return jnp.where(evolving[None, :], updated, current)
+
+    return with_layout_constraint(lax.fori_loop(0, STEPS, advance, current), Layout((0, 1)))
 
 
 def lane_gather(values, lanes):
@@ -95,10 +98,11 @@
 
 
 def interval_kernel(nd, nc, tiles, levels, block, pairs,
-                    tab, win, nbr, coef, mask, rows, state_hbm, cols_hbm, w_hbm,
-                    out_hbm,
+                    nbr, coef, mask, rows, sources, state_hbm, cols_hbm, w_hbm,
+                    out_hbm, flag_out,
                     pb0, pb1, pb2, pb3, pg0, pg1, pg2, pg3, outb, outg,
                     cols, wbuf, compact, slots, gsl, zslots, usl, sea, fpart, fgot, force,
+                    tabv, tab, flags, flags_in, tab_sem, gsend, grecv,
                     load_sem, w_sem, cols_sem, out_sem,
                     hsend, hrecv, asend, arecv, usend, urecv, ssend, srecv, fsend, frecv):
     comp = lax.axis_index("comp")
@@ -112,9 +116,10 @@
     right = lax.rem(dom + 1, nd)
     is_air = comp < ocean
     near_rel = [0, 1, 2, nd - 2, nd - 1]
-    T_WHICH, T_SEL, T_EXT, T_VALID = 0, nd, 2 * nd, 2 * nd + EXTRAS
-    T_NEARP = 2 * nd + 2 * EXTRAS
-    T_EP, T_EVALID, T_ESRC = T_NEARP + NEAR_COUNT, T_NEARP + NEAR_COUNT + 1, T_NEARP + NEAR_COUNT + 2
+    T_WHICH, T_SEL, T_EXT, T_VALID = 0, 1, 2, 2 + EXTRAS
+    T_NEARP = 2 + 2 * EXTRAS
+    T_EP = T_NEARP + NEAR_COUNT
+    T_EVALID, T_ESRC = T_EP + 1, T_EP + 2
 
     def load_g(j):
         return pltpu.make_async_copy(state_hbm.at[pl.ds(0, SUB), pl.ds(j * LANES, LANES)], pg0.at[j + halo], load_sem.at[0])
@@ -136,20 +141,97 @@
 
     barrier = pltpu.get_barrier_semaphore()
 
-    @pl.when(is_air)
-    def _():
-        def greet(r, _):
-            pl.semaphore_signal(barrier, inc=1, device_id=(comp, lax.rem(dom + r, nd)), device_id_type=MESH)
-            return 0
-        lax.fori_loop(1, nd, greet, 0)
-        pl.semaphore_signal(barrier, inc=1, device_id=(ocean, dom), device_id_type=MESH)
-
-    @pl.when(jnp.logical_not(is_air))
-    def _():
-        pl.semaphore_signal(barrier, inc=1, device_id=(comp, left), device_id_type=MESH)
-        pl.semaphore_signal(barrier, inc=1, device_id=(comp, right), device_id_type=MESH)
-        for c in range(ocean):
-            pl.semaphore_signal(barrier, inc=1, device_id=(c, dom), device_id_type=MESH)
+    def greet(r, _):
+        pl.semaphore_signal(barrier, inc=1, device_id=(comp, lax.rem(dom + r, nd)), device_id_type=MESH)
+        return 0
+    lax.fori_loop(1, nd, greet, 0)
+    for c in range(1, nc):
+        pl.semaphore_signal(barrier, inc=1, device_id=(lax.rem(comp + c, nc), dom), device_id_type=MESH)
+
+    def build_tables():
+        src = sources[...]
+        p_i = lax.broadcasted_iota(jnp.int32, (nd, pairs), 1)
+        t_i = lax.broadcasted_iota(jnp.int32, (nd, pairs), 0)
+        t_c = lax.broadcasted_iota(jnp.int32, (nd, 1), 0)
+        dom_f = dom
+        base = (comp * nd)
+
+        def is_far(offset):
+            offset = jnp.where(offset < 0, offset + nd, offset)
+            return jnp.logical_and(offset > NEAR, offset < nd - NEAR)
+
+        mine = src == base + dom_f
+        which = jnp.sum(jnp.where(mine, p_i, 0), axis=1, keepdims=True)
+        hit = jnp.max(jnp.where(mine, 1, 0), axis=1, keepdims=True)
+        far = jnp.where(jnp.logical_and(hit > 0, is_far(t_c - dom_f)), 1, 0)
+        lanes = [(T_WHICH, which)]
+        sel = jnp.zeros((nd, 1), jnp.int32)
+        last = jnp.full((1, 1), -1, jnp.int32)
+        for e in range(EXTRAS):
+            last = jnp.min(jnp.where(jnp.logical_and(far > 0, t_c > last), t_c, nd), axis=0, keepdims=True)
+            sel = jnp.where(t_c == last, e, sel)
+            lanes.append((T_EXT + e, last))
+            lanes.append((T_VALID + e, jnp.where(last < nd, 1, 0)))
+        lanes.append((T_SEL, sel))
+        crowded = jnp.sum(far, axis=0, keepdims=True) > EXTRAS
+
+        own = jnp.sum(jnp.where(t_i == dom_f, src, 0), axis=0, keepdims=True) - base
+        p_r = p_i[:1]
+        for n, r in enumerate(near_rel):
+            place = lax.rem(dom + r, nd)
+            lanes.append((T_NEARP + n, jnp.sum(jnp.where(own == place, p_r, 0), axis=1, keepdims=True)))
+        in_band = jnp.logical_and(own >= 0, own < nd)
+        far_own = jnp.where(jnp.logical_and(in_band, is_far(own - dom_f)), 1, 0)
+        lanes.append((T_EP, jnp.sum(far_own * p_r, axis=1, keepdims=True)))
+        lanes.append((T_EVALID, jnp.max(far_own, axis=1, keepdims=True)))
+        lanes.append((T_ESRC, jnp.sum(far_own * own, axis=1, keepdims=True)))
+        lane = lax.broadcasted_iota(jnp.int32, (nd, LANES), 1)
+        packed = jnp.zeros((nd, LANES), jnp.int32)
+        for at, value in lanes:
+            value = jnp.minimum(value, ((nd if at in (T_ESRC, *range(T_EXT, T_EXT + EXTRAS)) else pairs) - 1))
+            packed = jnp.where(lane == at, jnp.broadcast_to(value, (nd, LANES)), packed)
+        tabv[pl.ds(0, nd), :] = packed
+
+        reach = jnp.concatenate(
+            [nbr[:, j * LANES:(j + 1) * LANES] for j in range(tiles)], axis=0)
+        lane = lax.broadcasted_iota(jnp.int32, reach.shape, 1)
+        wide = jnp.zeros((1, 1), jnp.int32)
+        packed = jnp.zeros(reach.shape, jnp.int32)
+        for h, side in enumerate((lane < LANES // 2, lane >= LANES // 2)):
+            first = jnp.min(jnp.where(side, reach, 2**30), axis=1, keepdims=True)
+            first = jnp.clip(first, 0, ((tiles + 2 * halo - 1) * LANES))
+            final = jnp.max(jnp.where(side, reach, -1), axis=1, keepdims=True)
+            wide = jnp.maximum(wide, jnp.max(final - first, axis=0, keepdims=True))
+            packed = jnp.where(lane == h, jnp.broadcast_to(first, reach.shape), packed)
+        tabv[pl.ds(nd, EDGES * tiles), :] = packed
+        bad = jnp.logical_or(wide >= LANES, crowded)
+        flags[0] = jnp.broadcast_to(jnp.where(bad, 1.0, 0.0), (SUB, LANES))
+
+    build_tables()
+    to_smem = pltpu.make_async_copy(tabv, tab, tab_sem)
+    to_smem.start()
+
+    hops = []
+    reach_d = 1
+    while reach_d < nd:
+        hops.append((0, reach_d))
+        reach_d *= 2
+    reach_c = 1
+    while reach_c < nc:
+        hops.append((reach_c, 0))
+        reach_c *= 2
+
+    def flag_copy(i):
+        dc, dd = hops[i]
+        return pltpu.make_async_remote_copy(
+            src_ref=flags.at[i], dst_ref=flags_in.at[i], send_sem=gsend.at[i], recv_sem=grecv.at[i],
+            device_id=(lax.rem(comp + dc, nc), lax.rem(dom + dd, nd)), device_id_type=MESH)
+
+    def flag_next(i):
+        flag_copy(i).wait()
+        flags[i + 1] = jnp.maximum(flags[i], flags_in[i])
+        if i + 1 < len(hops):
+            flag_copy(i + 1).start()
 
     row8 = lax.broadcasted_iota(jnp.int32, (SUB, LANES), 0)
 
@@ -191,10 +273,11 @@
         return lax.dot_general(lhs, hot, (((1,), (1,)), ((), ())), preferred_element_type=F32)
 
     def cols_of(t):
-        return cols[t, pl.ds(tab[T_WHICH + t], 1), :]
+        return cols[t, pl.ds(tab[t, T_WHICH], 1), :]
 
     pltpu.make_async_copy(pg0.at[pl.ds(halo, tiles)], pg0.at[pl.ds(halo, tiles)], load_sem.at[0]).wait()
     cols_copy.wait()
+    to_smem.wait()
 
     @pl.when(is_air)
     def _():
@@ -209,7 +292,7 @@
                     slots[r, i] = acc
 
         def extra(e, _):
-            res = gather_slot(table, cols_of(tab[T_EXT + e]))
+            res = gather_slot(table, cols_of(tab[0, T_EXT + e]))
             for i, acc in enumerate(res):
                 compact[e, i] = acc
             return 0
@@ -217,17 +300,11 @@
 
         def fill(r, _):
             t = lax.rem(dom + r, nd)
-            slots[r] = compact[tab[T_SEL + t]]
+            slots[r] = compact[tab[t, T_SEL]]
             return 0
         lax.fori_loop(NEAR + 1, nd - NEAR, fill, 0)
 
-    @pl.when(is_air)
-    def _():
-        pl.semaphore_wait(barrier, nd)
-
-    @pl.when(jnp.logical_not(is_air))
-    def _():
-        pl.semaphore_wait(barrier, 2 + ocean)
+    pl.semaphore_wait(barrier, nd + nc - 2)
 
     def a_copy(r):
         return pltpu.make_async_remote_copy(
@@ -265,6 +342,7 @@
     pltpu.make_async_copy(pb0.at[pl.ds(halo, tiles)], pb0.at[pl.ds(halo, tiles)], load_sem.at[1]).wait()
     for c in halo_copies(pb[0], 0, 1):
         c.start()
+    flag_copy(0).start()
 
     lane1 = lax.broadcasted_iota(jnp.int32, (1, LANES), 1)
 
@@ -277,7 +355,7 @@
             lo = jnp.broadcast_to(nbr[pl.ds(k, 1), cols_j] & (LANES - 1), (rows_, LANES))
             got = []
             for h in range(2):
-                w = win[(k * tiles + j) * 2 + h]
+                w = tab[nd + j * EDGES + k, h]
                 b = jnp.minimum(w >> 7, tiles + 2 * halo - 2)
                 edge = jnp.broadcast_to(lane1 >= w - b * LANES, (rows_, LANES))
                 got.append(lane_gather(jnp.where(edge, src[b], src[b + 1]), lo))
@@ -291,7 +369,7 @@
     def bulk_step(s):
         src = pb[s]
         dst, off = (pb[s + 1], halo) if s + 1 < STEPS else (outb, 0)
-        per = 2
+        per = 4
 
         def body(i, _):
             new = [tile_step(src, i * per + u, bulk, False) for u in range(per)]
@@ -318,6 +396,7 @@
                 c.start()
 
     bulk_step(0)
+    flag_next(0)
 
     @pl.when(is_air)
     def _():
@@ -352,16 +431,16 @@
                 src_ref=zslots.at[slot], dst_ref=usl.at[dom], send_sem=usend, recv_sem=urecv,
                 device_id=(comp, lax.rem(dom + r, nd)), device_id_type=MESH)
 
-        eight, z, index = dense(tab[T_EP], tab[T_ESRC])
+        eight, z, index = dense(tab[0, T_EP], tab[0, T_ESRC])
         put(zslots, NEAR_COUNT, z)
 
         def send(r, _):
             u_copy(NEAR_COUNT, r).start()
             return 0
         lax.fori_loop(NEAR + 1, nd - NEAR, send, 0)
-        total = total + scatter(jnp.where(tab[T_EVALID] == 1, eight, 0.0), index)
+        total = total + scatter(jnp.where(tab[0, T_EVALID] == 1, eight, 0.0), index)
         for n, r in enumerate(near_rel):
-            eight, z, index = dense(tab[T_NEARP + n], lax.rem(dom + r, nd))
+            eight, z, index = dense(tab[0, T_NEARP + n], lax.rem(dom + r, nd))
             if r == 0:
                 put(usl, dom, z)
             else:
@@ -375,7 +454,9 @@
             src_ref=fpart, dst_ref=fgot.at[comp], send_sem=fsend, recv_sem=frecv,
             device_id=(ocean, dom), device_id_type=MESH).start()
 
+    flag_next(1)
     bulk_step(1)
+    flag_next(2)
 
     @pl.when(is_air)
     def _():
@@ -385,9 +466,9 @@
             t = lax.rem(dom + r, nd)
             total = total + scatter(split_rows([usl[t, i] for i in range(block // (2 * LANES))]), cols_of(t))
         for e in range(EXTRAS):
-            t = tab[T_EXT + e]
+            t = tab[0, T_EXT + e]
             eight = split_rows([usl[t, i] for i in range(block // (2 * LANES))])
-            total = total + scatter(jnp.where(tab[T_VALID + e] == 1, eight, 0.0), cols_of(t))
+            total = total + scatter(jnp.where(tab[0, T_VALID + e] == 1, eight, 0.0), cols_of(t))
         for h in range(tiles):
             part = total[h * SUB:(h + 1) * SUB]
             force[h] = part + pltpu.roll(part, FIELDS, axis=0)
@@ -399,8 +480,10 @@
             force[h] = fgot[0, h] + fgot[1, h] + fgot[2, h]
 
     group_step(0)
+    flag_next(3)
     bulk_step(2)
     group_step(1)
+    flag_next(4)
     bulk_step(3)
 
     def store_b(j):
@@ -411,7 +494,11 @@
 
     for j in range(tiles):
         store_b(j).start()
+    for i in range(5, len(hops) - 1):
+        flag_next(i)
     group_step(2)
+    flag_next(len(hops) - 1)
+    flag_out[...] = flags[len(hops)]
     group_step(3)
     for j in range(tiles):
         store_g(j).start()
@@ -430,7 +517,7 @@
     pltpu.make_async_copy(outg, outg, out_sem.at[0]).wait()
 
 
-def windowed(state, neighbors, edge_coef, sea_mask, pair_rows, pair_cols, remap_weight, table, windows):
+def windowed(state, neighbors, edge_coef, sea_mask, pair_rows, pair_cols, remap_weight, pair_source):
     nd, nc = lax.axis_size("dom"), lax.axis_size("comp")
     _, levels, columns = state.shape
     tiles = columns // LANES
@@ -438,7 +525,7 @@
     pairs, block = pair_rows.shape[1:]
     pieces = block // (2 * LANES)
     bulk = levels - SUB
-    smem = pl.BlockSpec(memory_space=pltpu.SMEM)
+    hops = (nd - 1).bit_length() + (nc - 1).bit_length()
     vmem = pl.BlockSpec(memory_space=pltpu.VMEM)
     hbm = pl.BlockSpec(memory_space=pl.ANY)
     dma = pltpu.SemaphoreType.DMA
@@ -459,63 +546,30 @@
             pltpu.VMEM((nc - 1, tiles, SUB, LANES), F32),
             pltpu.VMEM((tiles, SUB, LANES), F32),
         ]
+        + [pltpu.VMEM((nd + EDGES * tiles, LANES), jnp.int32), pltpu.SMEM((nd + EDGES * tiles, LANES), jnp.int32)]
+        + [pltpu.VMEM((hops + 1, SUB, LANES), F32), pltpu.VMEM((hops, SUB, LANES), F32), dma, dma((hops,)), dma((hops,))]
         + [dma((2,)), dma, dma, dma((2,))]
         + [dma((2, STEPS, 2)), dma((2, STEPS, 2))]
         + [dma] * 8
     )
     return pl.pallas_call(
         functools.partial(interval_kernel, nd, nc, tiles, levels, block, pairs),
-        out_shape=jax.ShapeDtypeStruct((levels, columns), F32),
-        in_specs=[smem, smem, vmem, vmem, vmem, vmem, hbm, hbm, hbm],
-        out_specs=hbm,
+        out_shape=[jax.ShapeDtypeStruct((levels, columns), F32), jax.ShapeDtypeStruct((SUB, LANES), F32)],
+        in_specs=[vmem] * 5 + [hbm] * 3,
+        out_specs=[hbm, vmem],
         scratch_shapes=scratch,
         name="interval",
         cost_estimate=pl.CostEstimate(flops=10**9, bytes_accessed=10**8, transcendentals=0),
         compiler_params=pltpu.CompilerParams(
-            collective_id=0, has_side_effects=True, vmem_limit_bytes=48 * 2**20),
-    )(table, windows, neighbors[0], edge_coef[0], sea_mask[None], pair_rows[0], state[0], pair_cols, remap_weight[0])
+            collective_id=0, has_side_effects=True, vmem_limit_bytes=60 * 2**20),
+    )(neighbors[0], edge_coef[0], sea_mask[None], pair_rows[0], pair_source, state[0], pair_cols, remap_weight[0])
 
 
 def local(state, neighbors, edge_coef, sea_mask, pair_source, pair_rows, pair_cols, remap_weight):
-    nd, nc = lax.axis_size("dom"), lax.axis_size("comp")
-    comp, dom = lax.axis_index("comp"), lax.axis_index("dom")
-    columns = state.shape[2]
-    tiles = columns // LANES
-    pairs = pair_source.shape[1]
-    i32 = jnp.int32
-
-    halves = neighbors[0].reshape(EDGES * tiles * 2, LANES // 2)
-    windows = jnp.minimum(jnp.min(halves, axis=1), columns + 2 * RIM - LANES)
-    wide = jnp.max(jnp.max(halves, axis=1) - windows) >= LANES
-
-    t = jnp.arange(nd, dtype=i32)
-    index = jnp.arange(pairs, dtype=i32)
-    matched = pair_source == comp * nd + dom
-    which = jnp.sum(jnp.where(matched, index[None], 0), axis=1).astype(i32)
-    offset = jnp.mod(t - dom, nd)
-    far = jnp.any(matched, axis=1) & (offset > NEAR) & (offset < nd - NEAR)
-    rank = jnp.cumsum(far.astype(i32)) - 1
-    sel = jnp.clip(jnp.where(far, rank, 0), 0, EXTRAS - 1).astype(i32)
-    hit = far[None] & (rank[None] == jnp.arange(EXTRAS, dtype=i32)[:, None])
-    ext = jnp.sum(jnp.where(hit, t[None], 0), axis=1).astype(i32)
-    valid = jnp.any(hit, axis=1).astype(i32)
-    crowded = jnp.sum(far.astype(i32)) > EXTRAS
-
-    own = lax.dynamic_index_in_dim(pair_source, dom, 0, keepdims=False)
-    own_offset = jnp.mod(own % nd - dom, nd)
-    own_band = own // nd == comp
-    rel = jnp.array([0, 1, 2, nd - 2, nd - 1], i32)
-    near_p = jnp.sum(jnp.where((own_offset[None] == rel[:, None]) & own_band[None], index[None], 0), axis=1).astype(i32)
-    own_far = (own_offset > NEAR) & (own_offset < nd - NEAR) & own_band
-    e_p = jnp.sum(jnp.where(own_far, index, 0)).astype(i32)
-    e_valid = jnp.any(own_far).astype(i32)
-    e_src = jnp.sum(jnp.where(own_far, own % nd, 0)).astype(i32)
-    table = jnp.concatenate([which, sel, ext, valid, near_p, jnp.stack([e_p, e_valid, e_src])])
-
-    bad = lax.psum(jnp.where(wide | crowded, 1.0, 0.0).astype(F32), ("comp", "dom")) > 0
-    fast = windowed(state, neighbors, edge_coef, sea_mask, pair_rows, pair_cols, remap_weight, table, windows)
+    fast, flags = windowed(state, neighbors, edge_coef, sea_mask, pair_rows, pair_cols, remap_weight, pair_source)
     args = (state, neighbors, edge_coef, sea_mask, pair_source, pair_rows, pair_cols, remap_weight)
-    return lax.cond(bad, lambda f, *a: general(*a), lambda f, *a: f, fast, *args)[None]
+    done = lax.while_loop(lambda c: c[0], lambda c: (False, general(*args)), (flags[0, 0] > 0, fast))
+    return done[1][None]
 
 
 def solution(mesh):

time: 131 us -> 58.2 us (0.44)
  blocking collectives: 63 us -> 0 us
  other arithmetic: 6.65 us -> 0 us
  between operations: 2.76 us -> 0.7 us
    psum x1 -> x0, blocking collectives: 63 us -> none  [local(): lax.psum(jnp.where(wide | crowded, 1.0, 0.0).astype(F32), ('comp', 'dom'))]
    reduce_sum x5 -> x0, other arithmetic: 3.1 us -> none  [the longest x1 0.84 us: local(): jnp.sum(jnp.where((own_offset[None] == rel[:, None]) & own_band[None], in...]
    unnamed x12 -> x8, local copies, waits for them, and re-layouts: 0.98 us -> 3.68 us
    pallas_call x1 -> x0, local copies, waits for them, and re-layouts: 1.55 us -> none
    concatenate x1 -> x0, local copies, waits for them, and re-layouts: 1.33 us -> none  [local(): jnp.concatenate([which, sel, ext, valid, near_p, jnp.stack([e_p, e_valid,...]
where the time goes in v2:
time: 58.2 us; the launch traced here: 57.9 us
  Pallas kernels  52.1 us (90%)
  local copies, waits for them, and re-layouts  4.86 us (8%)
  between operations  0.7 us (1%)
    pallas_call x1, Pallas kernels, windowed(): pl.pallas_call(functools.partial(interval_kernel, nd, nc, tiles, levels,...  52.1 us
    unnamed x8, local copies, waits for them, and re-layouts  3.68 us
    slice x1, local copies, waits for them, and re-layouts, local(): flags[0, 0] > 0  1.19 us

profile of v2, /device:TPU:0, one launch (start us, length us, event | category | flops | bytes accessed | tf_op | source)
XLA Modules:
  0.0 57.9 jit_solution(16319625392032703043)
XLA Ops:
  0.0 1.4 %copy.36.sources = s32[32,16]{1,0:T(8,128)} copy(s32[32,16]{0,1:T(8,128)} %param.18) | data formatting | bytes 4096 | tf_op args[4]
  1.4 0.0 copy-start.1
  1.4 0.0 copy-start.2
  1.4 0.0 copy-start.4
  1.4 52.1 %interval.1 = (f32[128,2048]{1,0:T(8,128)}, f32[8,128]{1,0:T(8,128)}) custom-call(s32[4,2048]{1,0:T(4,128)} %bitcast.132, f32[4,2048]{1,0:T(4,128)} %bitcast.135, s32[1,2048]{1,0:T(1,128)} %bitcast.152, s32[16,512]{1,0:T(8,128)} %bitcast.38.rows, s32[32,16]{1,0:T(8,128)} %copy.36.sources, f32[128,2048]{1,0:T(8,128)} %bitcast.39.state_hbm, ...), custom_call_target="tpu_custom_call" | custom-call | flops 1000000000 | bytes 100000000 | tf_op jit(solution)/shard_map/interval/pallas_call | solution.py:555
  53.5 1.2 %slice.114 = f32[1,1]{1,0:T(1,128)} slice(f32[8,128]{1,0:T(8,128)} %get-tuple-element.169), slice={[0:1], [0:1]} | slice | bytes 8 | tf_op jit(solution)/shard_map/slice | solution.py:571
  55.4 0.0 copy-done.1
  55.4 0.0 copy-done.2
  55.4 0.0 copy-done.4
  55.4 0.2 while.23
  55.6 2.3 %copy.64 = f32[1,128,2048]{2,1,0:T(8,128)} copy(f32[1,128,2048]{2,1,0:T(8,128)} %bitcast.151) | data formatting | bytes 2097152
Async XLA Ops:
  1.4 54.0 %copy-start.1 = (s32[1,4,2048]{2,1,0:T(4,128)S(1)}, s32[1,4,2048]{2,1,0:T(4,128)}, u32[]{:S(2)}) copy-start(s32[1,4,2048]{2,1,0:T(4,128)} %param.15) | copy-start | bytes 98308
  1.4 54.0 %copy-start.2 = (f32[1,4,2048]{2,1,0:T(4,128)S(1)}, f32[1,4,2048]{2,1,0:T(4,128)}, u32[]{:S(2)}) copy-start(f32[1,4,2048]{2,1,0:T(4,128)} %param.16) | copy-start | bytes 98308
  1.4 54.0 %copy-start.4 = (s32[2048]{0:T(1024)S(1)}, s32[2048]{0:T(1024)}, u32[]{:S(2)}) copy-start(s32[2048]{0:T(1024)} %param.17) | copy-start | bytes 24580

commit v3 on v2

--- a/solution.py
+++ b/solution.py
@@ -102,13 +102,14 @@
                     out_hbm, flag_out,
                     pb0, pb1, pb2, pb3, pg0, pg1, pg2, pg3, outb, outg,
                     cols, wbuf, compact, slots, gsl, zslots, usl, sea, fpart, fgot, force,
-                    tabv, tab, flags, flags_in, tab_sem, gsend, grecv,
+                    tabv, tab, flag, pflag, flags_in, tab_sem, gsend, grecv,
                     load_sem, w_sem, cols_sem, out_sem,
                     hsend, hrecv, asend, arecv, usend, urecv, ssend, srecv, fsend, frecv):
     comp = lax.axis_index("comp")
     dom = lax.axis_index("dom")
     ocean = nc - 1
     bulk = levels - SUB
+    pieces = block // (2 * LANES)
     halo = RIM // LANES
     pb = [pb0, pb1, pb2, pb3]
     pg = [pg0, pg1, pg2, pg3]
@@ -141,12 +142,23 @@
 
     barrier = pltpu.get_barrier_semaphore()
 
-    def greet(r, _):
-        pl.semaphore_signal(barrier, inc=1, device_id=(comp, lax.rem(dom + r, nd)), device_id_type=MESH)
-        return 0
-    lax.fori_loop(1, nd, greet, 0)
+    def greet(device):
+        pl.semaphore_signal(barrier, inc=1, device_id=device, device_id_type=MESH)
+
     for c in range(1, nc):
-        pl.semaphore_signal(barrier, inc=1, device_id=(lax.rem(comp + c, nc), dom), device_id_type=MESH)
+        greet((lax.rem(comp + c, nc), dom))
+
+    @pl.when(is_air)
+    def _():
+        def greet_plane(r, _):
+            greet((comp, lax.rem(dom + r, nd)))
+            return 0
+        lax.fori_loop(1, nd, greet_plane, 0)
+
+    @pl.when(jnp.logical_not(is_air))
+    def _():
+        greet((comp, left))
+        greet((comp, right))
 
     def build_tables():
         src = sources[...]
@@ -205,33 +217,12 @@
             packed = jnp.where(lane == h, jnp.broadcast_to(first, reach.shape), packed)
         tabv[pl.ds(nd, EDGES * tiles), :] = packed
         bad = jnp.logical_or(wide >= LANES, crowded)
-        flags[0] = jnp.broadcast_to(jnp.where(bad, 1.0, 0.0), (SUB, LANES))
+        mark = jnp.broadcast_to(jnp.where(bad, 1.0, 0.0), (SUB, LANES))
+        flag[...] = mark
 
     build_tables()
     to_smem = pltpu.make_async_copy(tabv, tab, tab_sem)
     to_smem.start()
-
-    hops = []
-    reach_d = 1
-    while reach_d < nd:
-        hops.append((0, reach_d))
-        reach_d *= 2
-    reach_c = 1
-    while reach_c < nc:
-        hops.append((reach_c, 0))
-        reach_c *= 2
-
-    def flag_copy(i):
-        dc, dd = hops[i]
-        return pltpu.make_async_remote_copy(
-            src_ref=flags.at[i], dst_ref=flags_in.at[i], send_sem=gsend.at[i], recv_sem=grecv.at[i],
-            device_id=(lax.rem(comp + dc, nc), lax.rem(dom + dd, nd)), device_id_type=MESH)
-
-    def flag_next(i):
-        flag_copy(i).wait()
-        flags[i + 1] = jnp.maximum(flags[i], flags_in[i])
-        if i + 1 < len(hops):
-            flag_copy(i + 1).start()
 
     row8 = lax.broadcasted_iota(jnp.int32, (SUB, LANES), 0)
 
@@ -304,7 +295,13 @@
             return 0
         lax.fori_loop(NEAR + 1, nd - NEAR, fill, 0)
 
-    pl.semaphore_wait(barrier, nd + nc - 2)
+    @pl.when(is_air)
+    def _():
+        pl.semaphore_wait(barrier, nd + nc - 2)
+
+    @pl.when(jnp.logical_not(is_air))
+    def _():
+        pl.semaphore_wait(barrier, nc + 1)
 
     def a_copy(r):
         return pltpu.make_async_remote_copy(
@@ -325,24 +322,41 @@
             src_ref=pg0.at[pl.ds(halo, tiles)], dst_ref=sea, send_sem=ssend, recv_sem=srecv,
             device_id=(c, dom), device_id_type=MESH)
 
+    def sea_flag_copy(c):
+        return pltpu.make_async_remote_copy(
+            src_ref=flag, dst_ref=flags_in.at[ocean], send_sem=gsend.at[0], recv_sem=grecv.at[0],
+            device_id=(c, dom), device_id_type=MESH)
+
+    def plane_flag_copy(c):
+        return pltpu.make_async_remote_copy(
+            src_ref=pflag, dst_ref=flags_in.at[comp], send_sem=gsend.at[1], recv_sem=grecv.at[1],
+            device_id=(lax.rem(comp + c, nc), dom), device_id_type=MESH)
+
+    def arrived(ref, sem):
+        pltpu.make_async_copy(ref, ref, sem).wait()
+
     @pl.when(jnp.logical_not(is_air))
     def _():
         for c in range(ocean):
             sea_copy(c).start()
-
-    @pl.when(is_air)
-    def _():
+        for c in range(ocean):
+            sea_flag_copy(c).start()
+
+    @pl.when(is_air)
+    def _():
+        for r in near_rel[1:]:
+            a_copy(r).start()
+
         def send(r, _):
             a_copy(r).start()
             return 0
-        lax.fori_loop(1, nd, send, 0)
+        lax.fori_loop(NEAR + 1, nd - NEAR, send, 0)
 
     for c in halo_copies(pg[0], 0, 0):
         c.start()
-    pltpu.make_async_copy(pb0.at[pl.ds(halo, tiles)], pb0.at[pl.ds(halo, tiles)], load_sem.at[1]).wait()
+    arrived(pb0.at[pl.ds(halo, tiles)], load_sem.at[1])
     for c in halo_copies(pb[0], 0, 1):
         c.start()
-    flag_copy(0).start()
 
     lane1 = lax.broadcasted_iota(jnp.int32, (1, LANES), 1)
 
@@ -395,14 +409,16 @@
             for c in halo_copies(pg[s + 1], s + 1, 0):
                 c.start()
 
-    bulk_step(0)
-    flag_next(0)
-
     @pl.when(is_air)
     def _():
         pltpu.make_async_copy(gsl.at[pl.ds(0, nd - 1)], gsl.at[pl.ds(0, nd - 1)], arecv).wait()
         pltpu.make_async_copy(sea, sea, srecv).wait()
         pltpu.make_async_copy(w_hbm, wbuf, w_sem).wait()
+        arrived(flag, grecv.at[0])
+        flag[...] = jnp.maximum(flag[...], flags_in[ocean])
+        for n in range(1, NEAR_COUNT + 1):
+            zslots[n, pieces] = flag[...]
+        usl[dom, pieces] = flag[...]
         sea_table = doubled(sea, 0)
         total = jnp.zeros((tiles * SUB, LANES), F32)
 
@@ -411,7 +427,7 @@
             wh = w.astype(BF16)
             wl = (w - wh.astype(F32)).astype(BF16)
             index = rows[pl.ds(p, 1), :]
-            x = split_rows([gsl[src, i] for i in range(block // (2 * LANES))]).astype(BF16)
+            x = split_rows([gsl[src, i] for i in range(pieces)]).astype(BF16)
             v = split_rows(gather_slot(sea_table, index)).astype(BF16)
             dims = (((1,), (1,)), ((), ()))
             y = (lax.dot_general(x, wh, dims, preferred_element_type=F32)
@@ -454,20 +470,22 @@
             src_ref=fpart, dst_ref=fgot.at[comp], send_sem=fsend, recv_sem=frecv,
             device_id=(ocean, dom), device_id_type=MESH).start()
 
-    flag_next(1)
-    bulk_step(1)
-    flag_next(2)
+    bulk_step(0)
 
     @pl.when(is_air)
     def _():
         pltpu.make_async_copy(usl.at[pl.ds(0, nd - 1)], usl.at[pl.ds(0, nd - 1)], urecv).wait()
+        plane = usl[0, pieces]
+        for t in range(1, nd):
+            plane = jnp.maximum(plane, usl[t, pieces])
+        pflag[...] = plane
         total = jnp.zeros((tiles * SUB, LANES), F32)
         for r in near_rel:
             t = lax.rem(dom + r, nd)
-            total = total + scatter(split_rows([usl[t, i] for i in range(block // (2 * LANES))]), cols_of(t))
+            total = total + scatter(split_rows([usl[t, i] for i in range(pieces)]), cols_of(t))
         for e in range(EXTRAS):
             t = tab[0, T_EXT + e]
-            eight = split_rows([usl[t, i] for i in range(block // (2 * LANES))])
+            eight = split_rows([usl[t, i] for i in range(pieces)])
             total = total + scatter(jnp.where(tab[0, T_VALID + e] == 1, eight, 0.0), cols_of(t))
         for h in range(tiles):
             part = total[h * SUB:(h + 1) * SUB]
@@ -480,10 +498,16 @@
             force[h] = fgot[0, h] + fgot[1, h] + fgot[2, h]
 
     group_step(0)
-    flag_next(3)
+
+    @pl.when(is_air)
+    def _():
+        for c in range(1, nc):
+            plane_flag_copy(c).start()
+
+    bulk_step(1)
+    group_step(1)
     bulk_step(2)
-    group_step(1)
-    flag_next(4)
+    group_step(2)
     bulk_step(3)
 
     def store_b(j):
@@ -494,24 +518,37 @@
 
     for j in range(tiles):
         store_b(j).start()
-    for i in range(5, len(hops) - 1):
-        flag_next(i)
-    group_step(2)
-    flag_next(len(hops) - 1)
-    flag_out[...] = flags[len(hops)]
     group_step(3)
     for j in range(tiles):
         store_g(j).start()
 
     @pl.when(is_air)
     def _():
+        arrived(flags_in.at[pl.ds(0, ocean - 1)], grecv.at[1])
+        total = pflag[...]
+        for c in range(ocean):
+            total = jnp.maximum(total, jnp.where(comp == c, 0.0, flags_in[c]))
+        flag_out[...] = total
+
+    @pl.when(jnp.logical_not(is_air))
+    def _():
+        arrived(flags_in.at[pl.ds(0, ocean)], grecv.at[1])
+        total = flags_in[0]
+        for c in range(1, ocean):
+            total = jnp.maximum(total, flags_in[c])
+        flag_out[...] = total
+
+    @pl.when(is_air)
+    def _():
         pltpu.make_async_copy(slots.at[pl.ds(0, nd - 1)], slots.at[pl.ds(0, nd - 1)], asend).wait()
-        pltpu.make_async_copy(slots.at[pl.ds(0, nd - 1)], slots.at[pl.ds(0, nd - 1)], usend).wait()
-        pltpu.make_async_copy(fpart, fpart, fsend).wait()
+        arrived(usl.at[pl.ds(0, nd - 1)], usend)
+        arrived(fpart, fsend)
+        arrived(flags_in.at[pl.ds(0, ocean)], gsend.at[1])
 
     @pl.when(jnp.logical_not(is_air))
     def _():
-        pltpu.make_async_copy(fgot, fgot, ssend).wait()
+        arrived(fgot, ssend)
+        arrived(flags_in.at[pl.ds(0, ocean)], gsend.at[0])
 
     pltpu.make_async_copy(outb, outb, out_sem.at[1]).wait()
     pltpu.make_async_copy(outg, outg, out_sem.at[0]).wait()
@@ -525,7 +562,6 @@
     pairs, block = pair_rows.shape[1:]
     pieces = block // (2 * LANES)
     bulk = levels - SUB
-    hops = (nd - 1).bit_length() + (nc - 1).bit_length()
     vmem = pl.BlockSpec(memory_space=pltpu.VMEM)
     hbm = pl.BlockSpec(memory_space=pl.ANY)
     dma = pltpu.SemaphoreType.DMA
@@ -539,15 +575,15 @@
             pltpu.VMEM((EXTRAS, pieces, SUB, LANES), F32),
             pltpu.VMEM((nd, pieces, SUB, LANES), F32),
             pltpu.VMEM((nd, pieces, SUB, LANES), F32),
-            pltpu.VMEM((NEAR_COUNT + 1, pieces, SUB, LANES), F32),
-            pltpu.VMEM((nd, pieces, SUB, LANES), F32),
+            pltpu.VMEM((NEAR_COUNT + 1, pieces + 1, SUB, LANES), F32),
+            pltpu.VMEM((nd, pieces + 1, SUB, LANES), F32),
             pltpu.VMEM((tiles, SUB, LANES), F32),
             pltpu.VMEM((tiles, SUB, LANES), F32),
             pltpu.VMEM((nc - 1, tiles, SUB, LANES), F32),
             pltpu.VMEM((tiles, SUB, LANES), F32),
         ]
         + [pltpu.VMEM((nd + EDGES * tiles, LANES), jnp.int32), pltpu.SMEM((nd + EDGES * tiles, LANES), jnp.int32)]
-        + [pltpu.VMEM((hops + 1, SUB, LANES), F32), pltpu.VMEM((hops, SUB, LANES), F32), dma, dma((hops,)), dma((hops,))]
+        + [pltpu.VMEM((SUB, LANES), F32)] * 2 + [pltpu.VMEM((nc, SUB, LANES), F32), dma, dma((2,)), dma((2,))]
         + [dma((2,)), dma, dma, dma((2,))]
         + [dma((2, STEPS, 2)), dma((2, STEPS, 2))]
         + [dma] * 8

time: 58.2 us -> 54.4 us (0.935)
  Pallas kernels: 52.1 us -> 48.3 us
    pallas_call x1, Pallas kernels: 52.1 us -> 48.3 us  [windowed(): pl.pallas_call(functools.partial(interval_kernel, nd, nc, tiles, levels,...]
where the time goes in v3:
time: 54.4 us; the launch traced here: 54.1 us
  Pallas kernels  48.3 us (89%)
  local copies, waits for them, and re-layouts  4.86 us (9%)
  between operations  0.7 us (1%)
    pallas_call x1, Pallas kernels, windowed(): pl.pallas_call(functools.partial(interval_kernel, nd, nc, tiles, levels,...  48.3 us
    unnamed x8, local copies, waits for them, and re-layouts  3.68 us
    slice x1, local copies, waits for them, and re-layouts, local(): flags[0, 0] > 0  1.19 us

profile of v3, /device:TPU:0, one launch (start us, length us, event | category | flops | bytes accessed | tf_op | source)
XLA Modules:
  0.0 54.1 jit_solution(9358277001966828198)
XLA Ops:
  0.0 1.4 %copy.36.sources = s32[32,16]{1,0:T(8,128)} copy(s32[32,16]{0,1:T(8,128)} %param.18) | data formatting | bytes 4096 | tf_op args[4]
  1.4 0.0 copy-start.1
  1.4 0.0 copy-start.2
  1.4 0.0 copy-start.4
  1.4 48.3 %interval.1 = (f32[128,2048]{1,0:T(8,128)}, f32[8,128]{1,0:T(8,128)}) custom-call(s32[4,2048]{1,0:T(4,128)} %bitcast.132, f32[4,2048]{1,0:T(4,128)} %bitcast.135, s32[1,2048]{1,0:T(1,128)} %bitcast.152, s32[16,512]{1,0:T(8,128)} %bitcast.38.rows, s32[32,16]{1,0:T(8,128)} %copy.36.sources, f32[128,2048]{1,0:T(8,128)} %bitcast.39.state_hbm, ...), custom_call_target="tpu_custom_call" | custom-call | flops 1000000000 | bytes 100000000 | tf_op jit(solution)/shard_map/interval/pallas_call | solution.py:591
  49.7 1.2 %slice.114 = f32[1,1]{1,0:T(1,128)} slice(f32[8,128]{1,0:T(8,128)} %get-tuple-element.169), slice={[0:1], [0:1]} | slice | bytes 8 | tf_op jit(solution)/shard_map/slice | solution.py:607
  51.6 0.0 copy-done.1
  51.6 0.0 copy-done.2
  51.6 0.0 copy-done.4
  51.6 0.2 while.23
  51.8 2.3 %copy.64 = f32[1,128,2048]{2,1,0:T(8,128)} copy(f32[1,128,2048]{2,1,0:T(8,128)} %bitcast.151) | data formatting | bytes 2097152
Async XLA Ops:
  1.4 50.2 %copy-start.1 = (s32[1,4,2048]{2,1,0:T(4,128)S(1)}, s32[1,4,2048]{2,1,0:T(4,128)}, u32[]{:S(2)}) copy-start(s32[1,4,2048]{2,1,0:T(4,128)} %param.15) | copy-start | bytes 98308
  1.4 50.2 %copy-start.2 = (f32[1,4,2048]{2,1,0:T(4,128)S(1)}, f32[1,4,2048]{2,1,0:T(4,128)}, u32[]{:S(2)}) copy-start(f32[1,4,2048]{2,1,0:T(4,128)} %param.16) | copy-start | bytes 98308
  1.4 50.2 %copy-start.4 = (s32[2048]{0:T(1024)S(1)}, s32[2048]{0:T(1024)}, u32[]{:S(2)}) copy-start(s32[2048]{0:T(1024)} %param.17) | copy-start | bytes 24580

commit v4 on v3

--- a/solution.py
+++ b/solution.py
@@ -99,11 +99,11 @@
 
 def interval_kernel(nd, nc, tiles, levels, block, pairs,
                     nbr, coef, mask, rows, sources, state_hbm, cols_hbm, w_hbm,
-                    out_hbm, flag_out,
-                    pb0, pb1, pb2, pb3, pg0, pg1, pg2, pg3, outb, outg,
+                    out, flag_out,
+                    pb0, pb1, pb2, pb3, pg0, pg1, pg2, pg3,
                     cols, wbuf, compact, slots, gsl, zslots, usl, sea, fpart, fgot, force,
                     tabv, tab, flag, pflag, flags_in, tab_sem, gsend, grecv,
-                    load_sem, w_sem, cols_sem, out_sem,
+                    load_sem, w_sem, cols_sem,
                     hsend, hrecv, asend, arecv, usend, urecv, ssend, srecv, fsend, frecv):
     comp = lax.axis_index("comp")
     dom = lax.axis_index("dom")
@@ -161,7 +161,7 @@
         greet((comp, right))
 
     def build_tables():
-        src = sources[...]
+        src = sources[...].T
         p_i = lax.broadcasted_iota(jnp.int32, (nd, pairs), 1)
         t_i = lax.broadcasted_iota(jnp.int32, (nd, pairs), 0)
         t_c = lax.broadcasted_iota(jnp.int32, (nd, 1), 0)
@@ -380,15 +380,20 @@
         keep = jnp.logical_or(is_air, mask[:, cols_j] == 1)
         return jnp.where(jnp.broadcast_to(keep, (rows_, LANES)), upd, cur)
 
+    def put_tile(bufs, s, j, levels_, value):
+        if s + 1 < STEPS:
+            bufs[s + 1][j + halo] = value
+        else:
+            out[levels_, pl.ds(pl.multiple_of(j * LANES, LANES), LANES)] = value
+
     def bulk_step(s):
         src = pb[s]
-        dst, off = (pb[s + 1], halo) if s + 1 < STEPS else (outb, 0)
         per = 4
 
         def body(i, _):
             new = [tile_step(src, i * per + u, bulk, False) for u in range(per)]
             for u in range(per):
-                dst[i * per + u + off] = new[u]
+                put_tile(pb, s, i * per + u, pl.ds(SUB, bulk), new[u])
             return 0
         for c in halo_copies(src, s, 1):
             c.wait()
@@ -399,15 +404,16 @@
 
     def group_step(s):
         src = pg[s]
-        dst, off = (pg[s + 1], halo) if s + 1 < STEPS else (outg, 0)
         for c in halo_copies(src, s, 0):
             c.wait()
         new = [tile_step(src, j, SUB, True) for j in range(tiles)]
         for j in range(tiles):
-            dst[j + off] = new[j]
+            put_tile(pg, s, j, pl.ds(0, SUB), new[j])
         if s + 1 < STEPS:
             for c in halo_copies(pg[s + 1], s + 1, 0):
                 c.start()
+
+    bulk_step(0)
 
     @pl.when(is_air)
     def _():
@@ -470,7 +476,7 @@
             src_ref=fpart, dst_ref=fgot.at[comp], send_sem=fsend, recv_sem=frecv,
             device_id=(ocean, dom), device_id_type=MESH).start()
 
-    bulk_step(0)
+    bulk_step(1)
 
     @pl.when(is_air)
     def _():
@@ -504,23 +510,11 @@
         for c in range(1, nc):
             plane_flag_copy(c).start()
 
-    bulk_step(1)
+    bulk_step(2)
     group_step(1)
-    bulk_step(2)
+    bulk_step(3)
     group_step(2)
-    bulk_step(3)
-
-    def store_b(j):
-        return pltpu.make_async_copy(outb.at[j], out_hbm.at[pl.ds(SUB, bulk), pl.ds(j * LANES, LANES)], out_sem.at[1])
-
-    def store_g(j):
-        return pltpu.make_async_copy(outg.at[j], out_hbm.at[pl.ds(0, SUB), pl.ds(j * LANES, LANES)], out_sem.at[0])
-
-    for j in range(tiles):
-        store_b(j).start()
     group_step(3)
-    for j in range(tiles):
-        store_g(j).start()
 
     @pl.when(is_air)
     def _():
@@ -550,11 +544,8 @@
         arrived(fgot, ssend)
         arrived(flags_in.at[pl.ds(0, ocean)], gsend.at[0])
 
-    pltpu.make_async_copy(outb, outb, out_sem.at[1]).wait()
-    pltpu.make_async_copy(outg, outg, out_sem.at[0]).wait()
-
-
-def windowed(state, neighbors, edge_coef, sea_mask, pair_rows, pair_cols, remap_weight, pair_source):
+
+def windowed(state, neighbors, edge_coef, sea_mask, pair_rows, pair_cols, remap_weight, sources):
     nd, nc = lax.axis_size("dom"), lax.axis_size("comp")
     _, levels, columns = state.shape
     tiles = columns // LANES
@@ -563,12 +554,11 @@
     pieces = block // (2 * LANES)
     bulk = levels - SUB
     vmem = pl.BlockSpec(memory_space=pltpu.VMEM)
-    hbm = pl.BlockSpec(memory_space=pl.ANY)
+    hbm = pl.BlockSpec(memory_space=pltpu.HBM)
     dma = pltpu.SemaphoreType.DMA
     scratch = (
         [pltpu.VMEM((padded, bulk, LANES), F32)] * STEPS
         + [pltpu.VMEM((padded, SUB, LANES), F32)] * STEPS
-        + [pltpu.VMEM((tiles, bulk, LANES), F32), pltpu.VMEM((tiles, SUB, LANES), F32)]
         + [
             pltpu.VMEM(pair_cols.shape, jnp.int32),
             pltpu.VMEM((pairs, block, block), F32),
@@ -584,7 +574,7 @@
         ]
         + [pltpu.VMEM((nd + EDGES * tiles, LANES), jnp.int32), pltpu.SMEM((nd + EDGES * tiles, LANES), jnp.int32)]
         + [pltpu.VMEM((SUB, LANES), F32)] * 2 + [pltpu.VMEM((nc, SUB, LANES), F32), dma, dma((2,)), dma((2,))]
-        + [dma((2,)), dma, dma, dma((2,))]
+        + [dma((2,)), dma, dma]
         + [dma((2, STEPS, 2)), dma((2, STEPS, 2))]
         + [dma] * 8
     )
@@ -592,20 +582,47 @@
         functools.partial(interval_kernel, nd, nc, tiles, levels, block, pairs),
         out_shape=[jax.ShapeDtypeStruct((levels, columns), F32), jax.ShapeDtypeStruct((SUB, LANES), F32)],
         in_specs=[vmem] * 5 + [hbm] * 3,
-        out_specs=[hbm, vmem],
+        out_specs=[vmem, vmem],
         scratch_shapes=scratch,
         name="interval",
         cost_estimate=pl.CostEstimate(flops=10**9, bytes_accessed=10**8, transcendentals=0),
         compiler_params=pltpu.CompilerParams(
-            collective_id=0, has_side_effects=True, vmem_limit_bytes=60 * 2**20),
-    )(neighbors[0], edge_coef[0], sea_mask[None], pair_rows[0], pair_source, state[0], pair_cols, remap_weight[0])
+            collective_id=0, has_side_effects=True, vmem_limit_bytes=57 * 2**20),
+    )(neighbors[0], edge_coef[0], sea_mask[None], pair_rows[0], sources, state[0], pair_cols, remap_weight[0])
+
+
+def publish_kernel(parts, source, result, sems):
+    rows = source.shape[0] // parts
+
+    def part(i):
+        at = pl.ds(i * rows, rows)
+        return pltpu.make_async_copy(source.at[at], result.at[at], sems.at[i])
+    for i in range(parts):
+        part(i).start()
+    for i in range(parts):
+        part(i).wait()
+
+
+def publish(array, parts=8):
+    return pl.pallas_call(
+        functools.partial(publish_kernel, parts),
+        out_shape=jax.ShapeDtypeStruct(array.shape, array.dtype),
+        in_specs=[pl.BlockSpec(memory_space=pl.ANY)],
+        out_specs=pl.BlockSpec(memory_space=pl.ANY),
+        scratch_shapes=[pltpu.SemaphoreType.DMA((parts,))],
+        name="publish",
+    )(array)
 
 
 def local(state, neighbors, edge_coef, sea_mask, pair_source, pair_rows, pair_cols, remap_weight):
-    fast, flags = windowed(state, neighbors, edge_coef, sea_mask, pair_rows, pair_cols, remap_weight, pair_source)
-    args = (state, neighbors, edge_coef, sea_mask, pair_source, pair_rows, pair_cols, remap_weight)
-    done = lax.while_loop(lambda c: c[0], lambda c: (False, general(*args)), (flags[0, 0] > 0, fast))
-    return done[1][None]
+    sources = lax.optimization_barrier(pair_source.T)
+    fast, flags = windowed(state, neighbors, edge_coef, sea_mask, pair_rows, pair_cols, remap_weight, sources)
+
+    def anyway(_):
+        return False, general(state, neighbors, edge_coef, sea_mask, sources.T, pair_rows, pair_cols, remap_weight)
+
+    done = lax.while_loop(lambda c: c[0], anyway, (flags[0, 0] > 0, fast))
+    return publish(done[1])[None]
 
 
 def solution(mesh):

time: 54.4 us -> 88.7 us (1.63)
  Pallas kernels: 48.3 us -> 85.5 us
  local copies, waits for them, and re-layouts: 4.86 us -> 1.88 us
    pallas_call x0 -> x1, Pallas kernels: none -> 32.9 us  [publish(): pl.pallas_call(functools.partial(publish_kernel, parts), out_shape=jax.Sh...]
    pallas_call x1, Pallas kernels: 48.3 us -> 52.6 us  [windowed(): pl.pallas_call(functools.partial(interval_kernel, nd, nc, tiles, levels,...]
    unnamed x8, local copies, waits for them, and re-layouts: 3.68 us -> 0.01 us
where the time goes in v4:
time: 88.7 us; the launch traced here: 88.5 us
  Pallas kernels  85.5 us (96%)
  local copies, waits for them, and re-layouts  1.88 us (2%)
    pallas_call x1, Pallas kernels, windowed(): pl.pallas_call(functools.partial(interval_kernel, nd, nc, tiles, levels,...  52.6 us
    pallas_call x1, Pallas kernels, publish(): pl.pallas_call(functools.partial(publish_kernel, parts), out_shape=jax.Sh...  32.9 us

profile of v4, /device:TPU:0, one launch (start us, length us, event | category | flops | bytes accessed | tf_op | source)
XLA Modules:
  0.0 88.5 jit_solution(16459923033787931846)
XLA Ops:
  0.0 0.0 copy-start.6
  0.0 0.0 copy-start.1
  0.0 0.0 copy-start.2
  0.0 0.0 copy-start.4
  0.0 52.6 %interval.1 = (f32[128,2048]{1,0:T(8,128)}, f32[8,128]{1,0:T(8,128)}) custom-call(s32[4,2048]{1,0:T(4,128)} %bitcast.132, f32[4,2048]{1,0:T(4,128)} %bitcast.135, s32[1,2048]{1,0:T(1,128)} %bitcast.152, s32[16,512]{1,0:T(8,128)} %bitcast.38.rows, s32[16,32]{1,0:T(8,128)} %bitcast.153, f32[128,2048]{1,0:T(8,128)} %bitcast.40.state_hbm, ...), custom_call_target="tpu_custom_call" | custom-call | flops 1000000000 | bytes 100000000 | tf_op jit(solution)/shard_map/interval/pallas_call | solution.py:581
  52.6 1.2 %slice.114 = f32[1,1]{1,0:T(1,128)} slice(f32[8,128]{1,0:T(8,128)} %get-tuple-element.169), slice={[0:1], [0:1]} | slice | bytes 8 | tf_op jit(solution)/shard_map/slice | solution.py:624
  54.4 0.0 copy-done.6
  54.5 0.7 copy.34
  55.1 0.0 copy-done.1
  55.1 0.0 copy-done.2
  55.1 0.0 copy-done.4
  55.1 0.2 while.23
  55.4 32.9 %publish.1 = f32[128,2048]{1,0:T(8,128)} custom-call(f32[128,2048]{1,0:T(8,128)} %get-tuple-element.416), custom_call_target="tpu_custom_call" | custom-call | tf_op jit(solution)/shard_map/publish/pallas_call | solution.py:607
Async XLA Ops:
  0.0 54.4 %copy-start.6 = (s32[32,16]{0,1:T(8,128)S(1)}, s32[32,16]{0,1:T(8,128)}, u32[]{:S(2)}) copy-start(s32[32,16]{0,1:T(8,128)} %param.18) | copy-start | bytes 6148
  0.0 55.1 %copy-start.1 = (s32[1,4,2048]{2,1,0:T(4,128)S(1)}, s32[1,4,2048]{2,1,0:T(4,128)}, u32[]{:S(2)}) copy-start(s32[1,4,2048]{2,1,0:T(4,128)} %param.15) | copy-start | bytes 98308
  0.0 55.1 %copy-start.2 = (f32[1,4,2048]{2,1,0:T(4,128)S(1)}, f32[1,4,2048]{2,1,0:T(4,128)}, u32[]{:S(2)}) copy-start(f32[1,4,2048]{2,1,0:T(4,128)} %param.16) | copy-start | bytes 98308
  0.0 55.1 %copy-start.4 = (s32[2048]{0:T(1024)S(1)}, s32[2048]{0:T(1024)}, u32[]{:S(2)}) copy-start(s32[2048]{0:T(1024)} %param.17) | copy-start | bytes 24580

commit v5 on v4

--- a/solution.py
+++ b/solution.py
@@ -100,10 +100,10 @@
 def interval_kernel(nd, nc, tiles, levels, block, pairs,
                     nbr, coef, mask, rows, sources, state_hbm, cols_hbm, w_hbm,
                     out, flag_out,
-                    pb0, pb1, pb2, pb3, pg0, pg1, pg2, pg3,
+                    pb0, pb1, pb2, pb3, pg0, pg1, pg2, pg3, outb, outg,
                     cols, wbuf, compact, slots, gsl, zslots, usl, sea, fpart, fgot, force,
                     tabv, tab, flag, pflag, flags_in, tab_sem, gsend, grecv,
-                    load_sem, w_sem, cols_sem,
+                    load_sem, w_sem, cols_sem, out_sem,
                     hsend, hrecv, asend, arecv, usend, urecv, ssend, srecv, fsend, frecv):
     comp = lax.axis_index("comp")
     dom = lax.axis_index("dom")
@@ -342,21 +342,24 @@
         for c in range(ocean):
             sea_flag_copy(c).start()
 
+    for c in halo_copies(pg[0], 0, 0):
+        c.start()
+
     @pl.when(is_air)
     def _():
         for r in near_rel[1:]:
             a_copy(r).start()
 
+    arrived(pb0.at[pl.ds(halo, tiles)], load_sem.at[1])
+    for c in halo_copies(pb[0], 0, 1):
+        c.start()
+
+    @pl.when(is_air)
+    def _():
         def send(r, _):
             a_copy(r).start()
             return 0
         lax.fori_loop(NEAR + 1, nd - NEAR, send, 0)
-
-    for c in halo_copies(pg[0], 0, 0):
-        c.start()
-    arrived(pb0.at[pl.ds(halo, tiles)], load_sem.at[1])
-    for c in halo_copies(pb[0], 0, 1):
-        c.start()
 
     lane1 = lax.broadcasted_iota(jnp.int32, (1, LANES), 1)
 
@@ -380,27 +383,39 @@
         keep = jnp.logical_or(is_air, mask[:, cols_j] == 1)
         return jnp.where(jnp.broadcast_to(keep, (rows_, LANES)), upd, cur)
 
-    def put_tile(bufs, s, j, levels_, value):
+    def put_tile(bufs, last, s, j, value):
         if s + 1 < STEPS:
             bufs[s + 1][j + halo] = value
         else:
-            out[levels_, pl.ds(pl.multiple_of(j * LANES, LANES), LANES)] = value
-
-    def bulk_step(s):
-        src = pb[s]
-        per = 4
-
+            last[j] = value
+
+    def bulk_tiles(s, js):
+        new = [tile_step(pb[s], j, bulk, False) for j in js]
+        for j, value in zip(js, new):
+            put_tile(pb, outb, s, j, value)
+
+    per = 4
+
+    def bulk_inner(s, first, last):
         def body(i, _):
-            new = [tile_step(src, i * per + u, bulk, False) for u in range(per)]
-            for u in range(per):
-                put_tile(pb, s, i * per + u, pl.ds(SUB, bulk), new[u])
+            start = halo + i * per
+            bulk_tiles(s, [start + u for u in range(per)])
             return 0
-        for c in halo_copies(src, s, 1):
+        lax.fori_loop(first, last, body, 0)
+
+    def bulk_edges(s):
+        for c in halo_copies(pb[s], s, 1):
             c.wait()
-        lax.fori_loop(0, tiles // per, body, 0)
+        bulk_tiles(s, list(range(halo)) + list(range(tiles - halo, tiles)))
         if s + 1 < STEPS:
             for c in halo_copies(pb[s + 1], s + 1, 1):
                 c.start()
+
+    inner = (tiles - 2 * halo) // per
+
+    def bulk_step(s):
+        bulk_edges(s)
+        bulk_inner(s, 0, inner)
 
     def group_step(s):
         src = pg[s]
@@ -408,7 +423,7 @@
             c.wait()
         new = [tile_step(src, j, SUB, True) for j in range(tiles)]
         for j in range(tiles):
-            put_tile(pg, s, j, pl.ds(0, SUB), new[j])
+            put_tile(pg, outg, s, j, new[j])
         if s + 1 < STEPS:
             for c in halo_copies(pg[s + 1], s + 1, 0):
                 c.start()
@@ -512,9 +527,22 @@
 
     bulk_step(2)
     group_step(1)
-    bulk_step(3)
+    bulk_edges(3)
+    bulk_inner(3, 0, 1)
     group_step(2)
+    bulk_inner(3, 1, inner)
+
+    def store_b(j):
+        return pltpu.make_async_copy(outb.at[j], out.at[pl.ds(SUB, bulk), pl.ds(j * LANES, LANES)], out_sem.at[1])
+
+    def store_g(j):
+        return pltpu.make_async_copy(outg.at[j], out.at[pl.ds(0, SUB), pl.ds(j * LANES, LANES)], out_sem.at[0])
+
+    for j in range(tiles):
+        store_b(j).start()
     group_step(3)
+    for j in range(tiles):
+        store_g(j).start()
 
     @pl.when(is_air)
     def _():
@@ -543,6 +571,9 @@
     def _():
         arrived(fgot, ssend)
         arrived(flags_in.at[pl.ds(0, ocean)], gsend.at[0])
+
+    arrived(outb, out_sem.at[1])
+    arrived(outg, out_sem.at[0])
 
 
 def windowed(state, neighbors, edge_coef, sea_mask, pair_rows, pair_cols, remap_weight, sources):
@@ -559,6 +590,7 @@
     scratch = (
         [pltpu.VMEM((padded, bulk, LANES), F32)] * STEPS
         + [pltpu.VMEM((padded, SUB, LANES), F32)] * STEPS
+        + [pltpu.VMEM((tiles, bulk, LANES), F32), pltpu.VMEM((tiles, SUB, LANES), F32)]
         + [
             pltpu.VMEM(pair_cols.shape, jnp.int32),
             pltpu.VMEM((pairs, block, block), F32),
@@ -574,7 +606,7 @@
         ]
         + [pltpu.VMEM((nd + EDGES * tiles, LANES), jnp.int32), pltpu.SMEM((nd + EDGES * tiles, LANES), jnp.int32)]
         + [pltpu.VMEM((SUB, LANES), F32)] * 2 + [pltpu.VMEM((nc, SUB, LANES), F32), dma, dma((2,)), dma((2,))]
-        + [dma((2,)), dma, dma]
+        + [dma((2,)), dma, dma, dma((2,))]
         + [dma((2, STEPS, 2)), dma((2, STEPS, 2))]
         + [dma] * 8
     )
@@ -582,7 +614,7 @@
         functools.partial(interval_kernel, nd, nc, tiles, levels, block, pairs),
         out_shape=[jax.ShapeDtypeStruct((levels, columns), F32), jax.ShapeDtypeStruct((SUB, LANES), F32)],
         in_specs=[vmem] * 5 + [hbm] * 3,
-        out_specs=[vmem, vmem],
+        out_specs=[hbm, vmem],
         scratch_shapes=scratch,
         name="interval",
         cost_estimate=pl.CostEstimate(flops=10**9, bytes_accessed=10**8, transcendentals=0),
@@ -591,25 +623,18 @@
     )(neighbors[0], edge_coef[0], sea_mask[None], pair_rows[0], sources, state[0], pair_cols, remap_weight[0])
 
 
-def publish_kernel(parts, source, result, sems):
-    rows = source.shape[0] // parts
-
-    def part(i):
-        at = pl.ds(i * rows, rows)
-        return pltpu.make_async_copy(source.at[at], result.at[at], sems.at[i])
-    for i in range(parts):
-        part(i).start()
-    for i in range(parts):
-        part(i).wait()
-
-
-def publish(array, parts=8):
+def publish_kernel(source, result):
+    result[...] = source[...]
+
+
+def publish(array, parts=4):
+    spec = pl.BlockSpec((array.shape[0] // parts, array.shape[1]), lambda i: (i, 0))
     return pl.pallas_call(
-        functools.partial(publish_kernel, parts),
+        publish_kernel,
         out_shape=jax.ShapeDtypeStruct(array.shape, array.dtype),
-        in_specs=[pl.BlockSpec(memory_space=pl.ANY)],
-        out_specs=pl.BlockSpec(memory_space=pl.ANY),
-        scratch_shapes=[pltpu.SemaphoreType.DMA((parts,))],
+        grid=(parts,),
+        in_specs=[spec],
+        out_specs=spec,
         name="publish",
     )(array)
 
@@ -619,7 +644,8 @@
     fast, flags = windowed(state, neighbors, edge_coef, sea_mask, pair_rows, pair_cols, remap_weight, sources)
 
     def anyway(_):
-        return False, general(state, neighbors, edge_coef, sea_mask, sources.T, pair_rows, pair_cols, remap_weight)
+        return False, general(state, neighbors, edge_coef, sea_mask,
+                              with_layout_constraint(sources, Layout((0, 1))).T, pair_rows, pair_cols, remap_weight)
 
     done = lax.while_loop(lambda c: c[0], anyway, (flags[0, 0] > 0, fast))
     return publish(done[1])[None]

time: 88.7 us -> 52.5 us (0.59)
  Pallas kernels: 85.5 us -> 50.1 us
    pallas_call x1, Pallas kernels: 32.9 us -> 3.37 us  [publish(): pl.pallas_call(publish_kernel, out_shape=jax.ShapeDtypeStruct(array.shape...]
    pallas_call x1, Pallas kernels: 52.6 us -> 46.8 us  [windowed(): pl.pallas_call(functools.partial(interval_kernel, nd, nc, tiles, levels,...]
where the time goes in v5:
time: 52.5 us; the launch traced here: 52.3 us
  Pallas kernels  50.1 us (95%)
  local copies, waits for them, and re-layouts  1.2 us (2%)
  between operations  0.7 us (1%)
    pallas_call x1, Pallas kernels, windowed(): pl.pallas_call(functools.partial(interval_kernel, nd, nc, tiles, levels,...  46.8 us
    pallas_call x1, Pallas kernels, publish(): pl.pallas_call(publish_kernel, out_shape=jax.ShapeDtypeStruct(array.shape...  3.37 us
    slice x1, local copies, waits for them, and re-layouts, local(): done = lax.while_loop(lambda c: c[0], anyway, (flags[0, 0] > 0, fast))  1.19 us

profile of v5, /device:TPU:0, one launch (start us, length us, event | category | flops | bytes accessed | tf_op | source)
XLA Modules:
  0.0 52.3 jit_solution(17247843821361121979)
XLA Ops:
  0.0 0.0 copy-start.1
  0.0 0.0 copy-start.2
  0.0 0.0 copy-start.4
  0.0 46.8 %interval.1 = (f32[128,2048]{1,0:T(8,128)}, f32[8,128]{1,0:T(8,128)}) custom-call(s32[4,2048]{1,0:T(4,128)} %bitcast.130, f32[4,2048]{1,0:T(4,128)} %bitcast.133, s32[1,2048]{1,0:T(1,128)} %bitcast.151, s32[16,512]{1,0:T(8,128)} %bitcast.37.rows, s32[16,32]{1,0:T(8,128)} %bitcast.149, f32[128,2048]{1,0:T(8,128)} %bitcast.39.state_hbm, ...), custom_call_target="tpu_custom_call" | custom-call | flops 1000000000 | bytes 100000000 | tf_op jit(solution)/shard_map/interval/pallas_call | solution.py:613
  46.8 1.2 %slice.114 = f32[1,1]{1,0:T(1,128)} slice(f32[8,128]{1,0:T(8,128)} %get-tuple-element.169), slice={[0:1], [0:1]} | slice | bytes 8 | tf_op jit(solution)/shard_map/slice | solution.py:650
  48.6 0.0 copy-done.1
  48.7 0.0 copy-done.2
  48.7 0.0 copy-done.4
  48.7 0.2 while.23
  48.9 3.4 %publish.1 = f32[128,2048]{1,0:T(8,128)} custom-call(f32[128,2048]{1,0:T(8,128)} %get-tuple-element.386), custom_call_target="tpu_custom_call" | custom-call | tf_op jit(solution)/shard_map/publish/pallas_call | solution.py:632
Async XLA Ops:
  0.0 48.6 %copy-start.1 = (s32[1,4,2048]{2,1,0:T(4,128)S(1)}, s32[1,4,2048]{2,1,0:T(4,128)}, u32[]{:S(2)}) copy-start(s32[1,4,2048]{2,1,0:T(4,128)} %param.15) | copy-start | bytes 98308
  0.0 48.6 %copy-start.2 = (f32[1,4,2048]{2,1,0:T(4,128)S(1)}, f32[1,4,2048]{2,1,0:T(4,128)}, u32[]{:S(2)}) copy-start(f32[1,4,2048]{2,1,0:T(4,128)} %param.16) | copy-start | bytes 98308
  0.0 48.7 %copy-start.4 = (s32[32,16]{0,1:T(8,128)S(1)}, s32[32,16]{0,1:T(8,128)}, u32[]{:S(2)}) copy-start(s32[32,16]{0,1:T(8,128)} %param.18) | copy-start | bytes 6148

commit v6 on v5

--- a/solution.py
+++ b/solution.py
@@ -101,7 +101,7 @@
                     nbr, coef, mask, rows, sources, state_hbm, cols_hbm, w_hbm,
                     out, flag_out,
                     pb0, pb1, pb2, pb3, pg0, pg1, pg2, pg3, outb, outg,
-                    cols, wbuf, compact, slots, gsl, zslots, usl, sea, fpart, fgot, force,
+                    cols, wbuf, compact, slots, gsl, zslots, usl, nslots, gnear, unear, sea, fpart, fgot, force,
                     tabv, tab, flag, pflag, flags_in, tab_sem, gsend, grecv,
                     load_sem, w_sem, cols_sem, out_sem,
                     hsend, hrecv, asend, arecv, usend, urecv, ssend, srecv, fsend, frecv):
@@ -117,6 +117,7 @@
     right = lax.rem(dom + 1, nd)
     is_air = comp < ocean
     near_rel = [0, 1, 2, nd - 2, nd - 1]
+    far_count = nd - NEAR_COUNT
     T_WHICH, T_SEL, T_EXT, T_VALID = 0, 1, 2, 2 + EXTRAS
     T_NEARP = 2 + 2 * EXTRAS
     T_EP = T_NEARP + NEAR_COUNT
@@ -273,14 +274,6 @@
     @pl.when(is_air)
     def _():
         table = doubled(pg0, halo)
-        for n, r in enumerate(near_rel):
-            t = lax.rem(dom + r, nd)
-            res = gather_slot(table, cols_of(t))
-            for i, acc in enumerate(res):
-                if r == 0:
-                    gsl[dom, i] = acc
-                else:
-                    slots[r, i] = acc
 
         def extra(e, _):
             res = gather_slot(table, cols_of(tab[0, T_EXT + e]))
@@ -303,10 +296,18 @@
     def _():
         pl.semaphore_wait(barrier, nc + 1)
 
+    def mirror(n):
+        return near_rel.index((nd - near_rel[n]) % nd)
+
     def a_copy(r):
         return pltpu.make_async_remote_copy(
-            src_ref=slots.at[r], dst_ref=gsl.at[dom], send_sem=asend, recv_sem=arecv,
+            src_ref=slots.at[r], dst_ref=gsl.at[dom], send_sem=asend.at[0], recv_sem=arecv.at[0],
             device_id=(comp, lax.rem(dom + r, nd)), device_id_type=MESH)
+
+    def a_near(n):
+        return pltpu.make_async_remote_copy(
+            src_ref=nslots.at[n], dst_ref=gnear.at[mirror(n)], send_sem=asend.at[1], recv_sem=arecv.at[1],
+            device_id=(comp, lax.rem(dom + near_rel[n], nd)), device_id_type=MESH)
 
     def halo_copies(ref, s, kind):
         to_left = pltpu.make_async_remote_copy(
@@ -342,14 +343,6 @@
         for c in range(ocean):
             sea_flag_copy(c).start()
 
-    for c in halo_copies(pg[0], 0, 0):
-        c.start()
-
-    @pl.when(is_air)
-    def _():
-        for r in near_rel[1:]:
-            a_copy(r).start()
-
     arrived(pb0.at[pl.ds(halo, tiles)], load_sem.at[1])
     for c in halo_copies(pb[0], 0, 1):
         c.start()
@@ -360,6 +353,19 @@
             a_copy(r).start()
             return 0
         lax.fori_loop(NEAR + 1, nd - NEAR, send, 0)
+        table = doubled(pg0, halo)
+        for n, r in enumerate(near_rel):
+            res = gather_slot(table, cols_of(lax.rem(dom + r, nd)))
+            for i, acc in enumerate(res):
+                if r == 0:
+                    gnear[n, i] = acc
+                else:
+                    nslots[n, i] = acc
+        for n in range(1, NEAR_COUNT):
+            a_near(n).start()
+
+    for c in halo_copies(pg[0], 0, 0):
+        c.start()
 
     lane1 = lax.broadcasted_iota(jnp.int32, (1, LANES), 1)
 
@@ -432,23 +438,20 @@
 
     @pl.when(is_air)
     def _():
-        pltpu.make_async_copy(gsl.at[pl.ds(0, nd - 1)], gsl.at[pl.ds(0, nd - 1)], arecv).wait()
-        pltpu.make_async_copy(sea, sea, srecv).wait()
+        arrived(sea, srecv)
+        arrived(flag, grecv.at[0])
         pltpu.make_async_copy(w_hbm, wbuf, w_sem).wait()
-        arrived(flag, grecv.at[0])
         flag[...] = jnp.maximum(flag[...], flags_in[ocean])
-        for n in range(1, NEAR_COUNT + 1):
+        for n in range(NEAR_COUNT + 1):
             zslots[n, pieces] = flag[...]
-        usl[dom, pieces] = flag[...]
         sea_table = doubled(sea, 0)
-        total = jnp.zeros((tiles * SUB, LANES), F32)
-
-        def dense(p, src):
+
+        def dense(p, slot):
             w = wbuf[p]
             wh = w.astype(BF16)
             wl = (w - wh.astype(F32)).astype(BF16)
             index = rows[pl.ds(p, 1), :]
-            x = split_rows([gsl[src, i] for i in range(pieces)]).astype(BF16)
+            x = split_rows(slot).astype(BF16)
             v = split_rows(gather_slot(sea_table, index)).astype(BF16)
             dims = (((1,), (1,)), ((), ()))
             y = (lax.dot_general(x, wh, dims, preferred_element_type=F32)
@@ -463,27 +466,42 @@
             for q in range(block // LANES):
                 ref[at, q // 2, pl.ds((q % 2) * FIELDS, FIELDS), :] = z[:, q * LANES:(q + 1) * LANES]
 
-        def u_copy(slot, r):
+        def u_copy(r):
             return pltpu.make_async_remote_copy(
-                src_ref=zslots.at[slot], dst_ref=usl.at[dom], send_sem=usend, recv_sem=urecv,
+                src_ref=zslots.at[NEAR_COUNT], dst_ref=usl.at[dom], send_sem=usend.at[0], recv_sem=urecv.at[0],
                 device_id=(comp, lax.rem(dom + r, nd)), device_id_type=MESH)
 
-        eight, z, index = dense(tab[0, T_EP], tab[0, T_ESRC])
+        def u_near(n):
+            return pltpu.make_async_remote_copy(
+                src_ref=zslots.at[n], dst_ref=unear.at[mirror(n)], send_sem=usend.at[1], recv_sem=urecv.at[1],
+                device_id=(comp, lax.rem(dom + near_rel[n], nd)), device_id_type=MESH)
+
+        def near_block(n):
+            eight, z, index = dense(tab[0, T_NEARP + n], [gnear[n, i] for i in range(pieces)])
+            if n == 0:
+                put(unear, n, z)
+            else:
+                put(zslots, n, z)
+                u_near(n).start()
+            return scatter(eight, index)
+
+        arrived(gnear.at[pl.ds(0, NEAR_COUNT - 1)], arecv.at[1])
+        total = near_block(1)
+        total = total + near_block(NEAR_COUNT - 1)
+
+        arrived(gsl.at[pl.ds(0, far_count)], arecv.at[0])
+        src = tab[0, T_ESRC]
+        eight, z, index = dense(tab[0, T_EP], [gsl[src, i] for i in range(pieces)])
         put(zslots, NEAR_COUNT, z)
 
         def send(r, _):
-            u_copy(NEAR_COUNT, r).start()
+            u_copy(r).start()
             return 0
         lax.fori_loop(NEAR + 1, nd - NEAR, send, 0)
         total = total + scatter(jnp.where(tab[0, T_EVALID] == 1, eight, 0.0), index)
-        for n, r in enumerate(near_rel):
-            eight, z, index = dense(tab[0, T_NEARP + n], lax.rem(dom + r, nd))
-            if r == 0:
-                put(usl, dom, z)
-            else:
-                put(zslots, n, z)
-                u_copy(n, r).start()
-            total = total + scatter(eight, index)
+        for n in range(2, NEAR_COUNT - 1):
+            total = total + near_block(n)
+        total = total + near_block(0)
         for h in range(tiles):
             part = total[h * SUB:(h + 1) * SUB]
             fpart[h] = part + pltpu.roll(part, FIELDS, axis=0)
@@ -495,15 +513,17 @@
 
     @pl.when(is_air)
     def _():
-        pltpu.make_async_copy(usl.at[pl.ds(0, nd - 1)], usl.at[pl.ds(0, nd - 1)], urecv).wait()
-        plane = usl[0, pieces]
-        for t in range(1, nd):
-            plane = jnp.maximum(plane, usl[t, pieces])
+        arrived(unear.at[pl.ds(0, NEAR_COUNT - 1)], urecv.at[1])
+        total = jnp.zeros((tiles * SUB, LANES), F32)
+        plane = flag[...]
+        for n, r in enumerate(near_rel):
+            if r:
+                plane = jnp.maximum(plane, unear[n, pieces])
+            total = total + scatter(split_rows([unear[n, i] for i in range(pieces)]), cols_of(lax.rem(dom + r, nd)))
+        arrived(usl.at[pl.ds(0, far_count)], urecv.at[0])
+        for r in range(NEAR + 1, nd - NEAR):
+            plane = jnp.maximum(plane, usl[lax.rem(dom + r, nd), pieces])
         pflag[...] = plane
-        total = jnp.zeros((tiles * SUB, LANES), F32)
-        for r in near_rel:
-            t = lax.rem(dom + r, nd)
-            total = total + scatter(split_rows([usl[t, i] for i in range(pieces)]), cols_of(t))
         for e in range(EXTRAS):
             t = tab[0, T_EXT + e]
             eight = split_rows([usl[t, i] for i in range(pieces)])
@@ -562,8 +582,10 @@
 
     @pl.when(is_air)
     def _():
-        pltpu.make_async_copy(slots.at[pl.ds(0, nd - 1)], slots.at[pl.ds(0, nd - 1)], asend).wait()
-        arrived(usl.at[pl.ds(0, nd - 1)], usend)
+        arrived(slots.at[pl.ds(0, far_count)], asend.at[0])
+        arrived(nslots.at[pl.ds(0, NEAR_COUNT - 1)], asend.at[1])
+        arrived(usl.at[pl.ds(0, far_count)], usend.at[0])
+        arrived(unear.at[pl.ds(0, NEAR_COUNT - 1)], usend.at[1])
         arrived(fpart, fsend)
         arrived(flags_in.at[pl.ds(0, ocean)], gsend.at[1])
 
@@ -599,6 +621,9 @@
             pltpu.VMEM((nd, pieces, SUB, LANES), F32),
             pltpu.VMEM((NEAR_COUNT + 1, pieces + 1, SUB, LANES), F32),
             pltpu.VMEM((nd, pieces + 1, SUB, LANES), F32),
+            pltpu.VMEM((NEAR_COUNT, pieces, SUB, LANES), F32),
+            pltpu.VMEM((NEAR_COUNT, pieces, SUB, LANES), F32),
+            pltpu.VMEM((NEAR_COUNT, pieces + 1, SUB, LANES), F32),
             pltpu.VMEM((tiles, SUB, LANES), F32),
             pltpu.VMEM((tiles, SUB, LANES), F32),
             pltpu.VMEM((nc - 1, tiles, SUB, LANES), F32),
@@ -608,7 +633,7 @@
         + [pltpu.VMEM((SUB, LANES), F32)] * 2 + [pltpu.VMEM((nc, SUB, LANES), F32), dma, dma((2,)), dma((2,))]
         + [dma((2,)), dma, dma, dma((2,))]
         + [dma((2, STEPS, 2)), dma((2, STEPS, 2))]
-        + [dma] * 8
+        + [dma((2,))] * 4 + [dma] * 4
     )
     return pl.pallas_call(
         functools.partial(interval_kernel, nd, nc, tiles, levels, block, pairs),
@@ -623,18 +648,33 @@
     )(neighbors[0], edge_coef[0], sea_mask[None], pair_rows[0], sources, state[0], pair_cols, remap_weight[0])
 
 
-def publish_kernel(source, result):
-    result[...] = source[...]
+def publish_kernel(parts, source, result, held, got, put):
+    rows = source.shape[0] // parts
+
+    def take(i):
+        at = pl.ds(i * rows, rows)
+        return pltpu.make_async_copy(source.at[at], held.at[at], got.at[i])
+
+    def give(i):
+        at = pl.ds(i * rows, rows)
+        return pltpu.make_async_copy(held.at[at], result.at[at], put.at[i])
+    for i in range(parts):
+        take(i).start()
+    for i in range(parts):
+        take(i).wait()
+        give(i).start()
+    for i in range(parts):
+        give(i).wait()
 
 
 def publish(array, parts=4):
-    spec = pl.BlockSpec((array.shape[0] // parts, array.shape[1]), lambda i: (i, 0))
+    hbm = pl.BlockSpec(memory_space=pltpu.HBM)
     return pl.pallas_call(
-        publish_kernel,
+        functools.partial(publish_kernel, parts),
         out_shape=jax.ShapeDtypeStruct(array.shape, array.dtype),
-        grid=(parts,),
-        in_specs=[spec],
-        out_specs=spec,
+        in_specs=[hbm],
+        out_specs=hbm,
+        scratch_shapes=[pltpu.VMEM(array.shape, array.dtype)] + [pltpu.SemaphoreType.DMA((parts,))] * 2,
         name="publish",
     )(array)
 

time: 52.5 us -> 48.5 us (0.924)
  Pallas kernels: 50.1 us -> 45.9 us
    pallas_call x1, Pallas kernels: 46.8 us -> 43.9 us  [windowed(): pl.pallas_call(functools.partial(interval_kernel, nd, nc, tiles, levels,...]
    pallas_call x1, Pallas kernels: 3.37 us -> 1.98 us  [publish(): pl.pallas_call(functools.partial(publish_kernel, parts), out_shape=jax.Sh...]
where the time goes in v6:
time: 48.5 us; the launch traced here: 48.2 us
  Pallas kernels  45.9 us (95%)
  local copies, waits for them, and re-layouts  1.2 us (2%)
  between operations  0.88 us (2%)
    pallas_call x1, Pallas kernels, windowed(): pl.pallas_call(functools.partial(interval_kernel, nd, nc, tiles, levels,...  43.9 us
    pallas_call x1, Pallas kernels, publish(): pl.pallas_call(functools.partial(publish_kernel, parts), out_shape=jax.Sh...  1.98 us
    slice x1, local copies, waits for them, and re-layouts, local(): done = lax.while_loop(lambda c: c[0], anyway, (flags[0, 0] > 0, fast))  1.19 us

profile of v6, /device:TPU:0, one launch (start us, length us, event | category | flops | bytes accessed | tf_op | source)
XLA Modules:
  0.0 48.2 jit_solution(10727581361321983267)
XLA Ops:
  0.0 0.0 copy-start.1
  0.0 0.0 copy-start.2
  0.0 0.0 copy-start.4
  0.0 43.9 %interval.1 = (f32[128,2048]{1,0:T(8,128)}, f32[8,128]{1,0:T(8,128)}) custom-call(s32[4,2048]{1,0:T(4,128)} %bitcast.130, f32[4,2048]{1,0:T(4,128)} %bitcast.133, s32[1,2048]{1,0:T(1,128)} %bitcast.151, s32[16,512]{1,0:T(8,128)} %bitcast.37.rows, s32[16,32]{1,0:T(8,128)} %bitcast.149, f32[128,2048]{1,0:T(8,128)} %bitcast.39.state_hbm, ...), custom_call_target="tpu_custom_call" | custom-call | flops 1000000000 | bytes 100000000 | tf_op jit(solution)/shard_map/interval/pallas_call | solution.py:638
  44.0 1.2 %slice.114 = f32[1,1]{1,0:T(1,128)} slice(f32[8,128]{1,0:T(8,128)} %get-tuple-element.169), slice={[0:1], [0:1]} | slice | bytes 8 | tf_op jit(solution)/shard_map/slice | solution.py:690
  45.8 0.0 copy-done.1
  45.8 0.0 copy-done.2
  45.8 0.0 copy-done.4
  45.8 0.2 while.23
  46.1 2.0 %publish.1 = f32[128,2048]{1,0:T(8,128)} custom-call(f32[128,2048]{1,0:T(8,128)} %get-tuple-element.386), custom_call_target="tpu_custom_call" | custom-call | tf_op jit(solution)/shard_map/publish/pallas_call | solution.py:672
Async XLA Ops:
  0.0 45.8 %copy-start.1 = (s32[1,4,2048]{2,1,0:T(4,128)S(1)}, s32[1,4,2048]{2,1,0:T(4,128)}, u32[]{:S(2)}) copy-start(s32[1,4,2048]{2,1,0:T(4,128)} %param.15) | copy-start | bytes 98308
  0.0 45.8 %copy-start.2 = (f32[1,4,2048]{2,1,0:T(4,128)S(1)}, f32[1,4,2048]{2,1,0:T(4,128)}, u32[]{:S(2)}) copy-start(f32[1,4,2048]{2,1,0:T(4,128)} %param.16) | copy-start | bytes 98308
  0.0 45.8 %copy-start.4 = (s32[32,16]{0,1:T(8,128)S(1)}, s32[32,16]{0,1:T(8,128)}, u32[]{:S(2)}) copy-start(s32[32,16]{0,1:T(8,128)} %param.18) | copy-start | bytes 6148

commit v7 on v6

--- a/solution.py
+++ b/solution.py
@@ -18,6 +18,9 @@
 SUB = 8
 NEAR = 2
 NEAR_COUNT = 2 * NEAR + 1
+CONE = 3
+RING = 8
+REACH = RING + CONE
 EXTRAS = 4
 MESH = pl.DeviceIdType.MESH
 F32 = jnp.float32
@@ -100,7 +103,7 @@
 def interval_kernel(nd, nc, tiles, levels, block, pairs,
                     nbr, coef, mask, rows, sources, state_hbm, cols_hbm, w_hbm,
                     out, flag_out,
-                    pb0, pb1, pb2, pb3, pg0, pg1, pg2, pg3, outb, outg,
+                    pb0, pb1, pb2, pb3, gx0, gx1, gx2, gx3, outb, outg, ix, cx, tabw, tab2,
                     cols, wbuf, compact, slots, gsl, zslots, usl, nslots, gnear, unear, sea, fpart, fgot, force,
                     tabv, tab, flag, pflag, flags_in, tab_sem, gsend, grecv,
                     load_sem, w_sem, cols_sem, out_sem,
@@ -112,7 +115,7 @@
     pieces = block // (2 * LANES)
     halo = RIM // LANES
     pb = [pb0, pb1, pb2, pb3]
-    pg = [pg0, pg1, pg2, pg3]
+    gx = [gx0, gx1, gx2, gx3]
     left = lax.rem(dom + nd - 1, nd)
     right = lax.rem(dom + 1, nd)
     is_air = comp < ocean
@@ -124,7 +127,7 @@
     T_EVALID, T_ESRC = T_EP + 1, T_EP + 2
 
     def load_g(j):
-        return pltpu.make_async_copy(state_hbm.at[pl.ds(0, SUB), pl.ds(j * LANES, LANES)], pg0.at[j + halo], load_sem.at[0])
+        return pltpu.make_async_copy(state_hbm.at[pl.ds(0, SUB), pl.ds(j * LANES, LANES)], gx0.at[j + REACH], load_sem.at[0])
 
     def load_b(j):
         return pltpu.make_async_copy(state_hbm.at[pl.ds(SUB, bulk), pl.ds(j * LANES, LANES)], pb0.at[j + halo], load_sem.at[1])
@@ -209,6 +212,7 @@
             [nbr[:, j * LANES:(j + 1) * LANES] for j in range(tiles)], axis=0)
         lane = lax.broadcasted_iota(jnp.int32, reach.shape, 1)
         wide = jnp.zeros((1, 1), jnp.int32)
+        stray = jnp.zeros((1, 1), jnp.int32)
         packed = jnp.zeros(reach.shape, jnp.int32)
         for h, side in enumerate((lane < LANES // 2, lane >= LANES // 2)):
             first = jnp.min(jnp.where(side, reach, 2**30), axis=1, keepdims=True)
@@ -216,12 +220,22 @@
             final = jnp.max(jnp.where(side, reach, -1), axis=1, keepdims=True)
             wide = jnp.maximum(wide, jnp.max(final - first, axis=0, keepdims=True))
             packed = jnp.where(lane == h, jnp.broadcast_to(first, reach.shape), packed)
+            tile = lax.broadcasted_iota(jnp.int32, first.shape, 0) // EDGES
+            place = jnp.minimum(first >> 7, tiles + 2 * halo - 2)
+            outside = jnp.logical_or(place < tile + halo - CONE, place + 1 > tile + halo + CONE)
+            stray = jnp.maximum(stray, jnp.max(jnp.where(outside, 1, 0), axis=0, keepdims=True))
         tabv[pl.ds(nd, EDGES * tiles), :] = packed
-        bad = jnp.logical_or(wide >= LANES, crowded)
+        bad = jnp.logical_or(jnp.logical_or(wide >= LANES, stray > 0), crowded)
         mark = jnp.broadcast_to(jnp.where(bad, 1.0, 0.0), (SUB, LANES))
         flag[...] = mark
 
     build_tables()
+    for j in range(tiles):
+        at = pl.ds(j * LANES, LANES)
+        ix[RING + j, pl.ds(0, EDGES), :] = nbr[:, at]
+        cx[RING + j, pl.ds(0, EDGES), :] = coef[:, at]
+        keep = jnp.logical_or(is_air, mask[:, at] == 1)
+        cx[RING + j, pl.ds(EDGES, 1), :] = jnp.where(keep, 1.0, 0.0)
     to_smem = pltpu.make_async_copy(tabv, tab, tab_sem)
     to_smem.start()
 
@@ -267,13 +281,13 @@
     def cols_of(t):
         return cols[t, pl.ds(tab[t, T_WHICH], 1), :]
 
-    pltpu.make_async_copy(pg0.at[pl.ds(halo, tiles)], pg0.at[pl.ds(halo, tiles)], load_sem.at[0]).wait()
+    pltpu.make_async_copy(gx0.at[pl.ds(REACH, tiles)], gx0.at[pl.ds(REACH, tiles)], load_sem.at[0]).wait()
     cols_copy.wait()
     to_smem.wait()
 
     @pl.when(is_air)
     def _():
-        table = doubled(pg0, halo)
+        table = doubled(gx0, REACH)
 
         def extra(e, _):
             res = gather_slot(table, cols_of(tab[0, T_EXT + e]))
@@ -318,9 +332,20 @@
             send_sem=hsend.at[kind, s, 1], recv_sem=hrecv.at[kind, s, 1], device_id=(comp, right), device_id_type=MESH)
         return to_left, to_right
 
+    def ring_copies(ref, width, i):
+        to_left = pltpu.make_async_remote_copy(
+            src_ref=ref.at[pl.ds(width, width)], dst_ref=ref.at[pl.ds(tiles + width, width)],
+            send_sem=hsend.at[0, i, 0], recv_sem=hrecv.at[0, i, 0], device_id=(comp, left), device_id_type=MESH)
+        to_right = pltpu.make_async_remote_copy(
+            src_ref=ref.at[pl.ds(tiles, width)], dst_ref=ref.at[pl.ds(0, width)],
+            send_sem=hsend.at[0, i, 1], recv_sem=hrecv.at[0, i, 1], device_id=(comp, right), device_id_type=MESH)
+        return to_left, to_right
+
+    early = [(gx0, REACH, 0), (ix, RING, 1), (cx, RING, 2)]
+
     def sea_copy(c):
         return pltpu.make_async_remote_copy(
-            src_ref=pg0.at[pl.ds(halo, tiles)], dst_ref=sea, send_sem=ssend, recv_sem=srecv,
+            src_ref=gx0.at[pl.ds(REACH, tiles)], dst_ref=sea, send_sem=ssend, recv_sem=srecv,
             device_id=(c, dom), device_id_type=MESH)
 
     def sea_flag_copy(c):
@@ -353,7 +378,7 @@
             a_copy(r).start()
             return 0
         lax.fori_loop(NEAR + 1, nd - NEAR, send, 0)
-        table = doubled(pg0, halo)
+        table = doubled(gx0, REACH)
         for n, r in enumerate(near_rel):
             res = gather_slot(table, cols_of(lax.rem(dom + r, nd)))
             for i, acc in enumerate(res):
@@ -364,12 +389,13 @@
         for n in range(1, NEAR_COUNT):
             a_near(n).start()
 
-    for c in halo_copies(pg[0], 0, 0):
-        c.start()
+    for ref, width, i in early:
+        for c in ring_copies(ref, width, i):
+            c.start()
 
     lane1 = lax.broadcasted_iota(jnp.int32, (1, LANES), 1)
 
-    def tile_step(src, j, rows_, forced):
+    def tile_step(src, j, rows_):
         cols_j = pl.ds(pl.multiple_of(j * LANES, LANES), LANES)
         cur = src[j + halo]
         upd = cur
@@ -383,22 +409,19 @@
                 edge = jnp.broadcast_to(lane1 >= w - b * LANES, (rows_, LANES))
                 got.append(lane_gather(jnp.where(edge, src[b], src[b + 1]), lo))
             upd = upd + coef[pl.ds(k, 1), cols_j] * (jnp.where(low, got[0], got[1]) - cur)
-        if forced:
-            gain = jnp.where(row8 < FIELDS, FORCE_GAIN, 0.0)
-            upd = upd + gain * (force[j] - cur)
         keep = jnp.logical_or(is_air, mask[:, cols_j] == 1)
         return jnp.where(jnp.broadcast_to(keep, (rows_, LANES)), upd, cur)
 
-    def put_tile(bufs, last, s, j, value):
+    def put_tile(s, j, value):
         if s + 1 < STEPS:
-            bufs[s + 1][j + halo] = value
+            pb[s + 1][j + halo] = value
         else:
-            last[j] = value
+            outb[j] = value
 
     def bulk_tiles(s, js):
-        new = [tile_step(pb[s], j, bulk, False) for j in js]
+        new = [tile_step(pb[s], j, bulk) for j in js]
         for j, value in zip(js, new):
-            put_tile(pb, outb, s, j, value)
+            put_tile(s, j, value)
 
     per = 4
 
@@ -423,16 +446,55 @@
         bulk_edges(s)
         bulk_inner(s, 0, inner)
 
-    def group_step(s):
-        src = pg[s]
-        for c in halo_copies(src, s, 0):
-            c.wait()
-        new = [tile_step(src, j, SUB, True) for j in range(tiles)]
-        for j in range(tiles):
-            put_tile(pg, outg, s, j, new[j])
-        if s + 1 < STEPS:
-            for c in halo_copies(pg[s + 1], s + 1, 0):
-                c.start()
+    def ring_windows():
+        for ref, width, i in early:
+            for c in ring_copies(ref, width, i):
+                c.wait()
+        reach = jnp.concatenate([ix[t, pl.ds(0, EDGES), :] for t in range(tiles + 2 * RING)], axis=0)
+        lane = lax.broadcasted_iota(jnp.int32, reach.shape, 1)
+        packed = jnp.zeros(reach.shape, jnp.int32)
+        for h, side in enumerate((lane < LANES // 2, lane >= LANES // 2)):
+            first = jnp.min(jnp.where(side, reach, 2**30), axis=1, keepdims=True)
+            first = jnp.clip(first, 0, (tiles + 2 * halo - 1) * LANES)
+            packed = jnp.where(lane == h, jnp.broadcast_to(first, reach.shape), packed)
+        tabw[...] = packed
+        pltpu.make_async_copy(tabw, tab2, tab_sem).start()
+
+    low8 = lane1 < LANES // 2
+    gain8 = jnp.where(row8 < FIELDS, FORCE_GAIN, 0.0)
+
+    def ring_tile(s, t):
+        src = gx[s]
+        cur = src[t + CONE]
+        upd = cur
+        shift = jnp.where(t < RING, -tiles, jnp.where(t >= RING + tiles, tiles, 0)) + (REACH - halo)
+        for k in range(EDGES):
+            lo = jnp.broadcast_to(ix[t, pl.ds(k, 1), :] & (LANES - 1), (SUB, LANES))
+            got = []
+            for h in range(2):
+                w = tab2[t * EDGES + k, h]
+                b = jnp.minimum(w >> 7, tiles + 2 * halo - 2)
+                edge = jnp.broadcast_to(lane1 >= w - b * LANES, (SUB, LANES))
+                at = jnp.clip(b + shift, 0, tiles + 2 * REACH - 2)
+                got.append(lane_gather(jnp.where(edge, src[at], src[at + 1]), lo))
+            upd = upd + cx[t, pl.ds(k, 1), :] * (jnp.where(low8, got[0], got[1]) - cur)
+        upd = upd + gain8 * (force[t] - cur)
+        return jnp.where(cx[t, pl.ds(EDGES, 1), :] > 0.5, upd, cur)
+
+    def ring_step(s):
+        spread = [RING, RING, RING // 2, 0][s]
+        many = 8
+
+        def body(i, _):
+            first = RING - spread + i * many
+            new = [ring_tile(s, first + u) for u in range(many)]
+            for u in range(many):
+                if s + 1 < STEPS:
+                    gx[s + 1][first + u + CONE] = new[u]
+                else:
+                    outg[first + u - RING] = new[u]
+            return 0
+        lax.fori_loop(0, (tiles + 2 * spread) // many, body, 0)
 
     bulk_step(0)
 
@@ -509,6 +571,7 @@
             src_ref=fpart, dst_ref=fgot.at[comp], send_sem=fsend, recv_sem=frecv,
             device_id=(ocean, dom), device_id_type=MESH).start()
 
+    ring_windows()
     bulk_step(1)
 
     @pl.when(is_air)
@@ -530,15 +593,22 @@
             total = total + scatter(jnp.where(tab[0, T_VALID + e] == 1, eight, 0.0), cols_of(t))
         for h in range(tiles):
             part = total[h * SUB:(h + 1) * SUB]
-            force[h] = part + pltpu.roll(part, FIELDS, axis=0)
+            force[RING + h] = part + pltpu.roll(part, FIELDS, axis=0)
 
     @pl.when(jnp.logical_not(is_air))
     def _():
         pltpu.make_async_copy(fgot, fgot, frecv).wait()
         for h in range(tiles):
-            force[h] = fgot[0, h] + fgot[1, h] + fgot[2, h]
-
-    group_step(0)
+            force[RING + h] = fgot[0, h] + fgot[1, h] + fgot[2, h]
+
+    def store_b(j):
+        return pltpu.make_async_copy(outb.at[j], out.at[pl.ds(SUB, bulk), pl.ds(j * LANES, LANES)], out_sem.at[1])
+
+    def store_g(j):
+        return pltpu.make_async_copy(outg.at[j], out.at[pl.ds(0, SUB), pl.ds(j * LANES, LANES)], out_sem.at[0])
+
+    for c in ring_copies(force, RING, 3):
+        c.start()
 
     @pl.when(is_air)
     def _():
@@ -546,23 +616,17 @@
             plane_flag_copy(c).start()
 
     bulk_step(2)
-    group_step(1)
-    bulk_edges(3)
-    bulk_inner(3, 0, 1)
-    group_step(2)
-    bulk_inner(3, 1, inner)
-
-    def store_b(j):
-        return pltpu.make_async_copy(outb.at[j], out.at[pl.ds(SUB, bulk), pl.ds(j * LANES, LANES)], out_sem.at[1])
-
-    def store_g(j):
-        return pltpu.make_async_copy(outg.at[j], out.at[pl.ds(0, SUB), pl.ds(j * LANES, LANES)], out_sem.at[0])
+    pltpu.make_async_copy(tabw, tab2, tab_sem).wait()
+    for c in ring_copies(force, RING, 3):
+        c.wait()
+    for s in range(STEPS):
+        ring_step(s)
+    for j in range(tiles):
+        store_g(j).start()
+    bulk_step(3)
 
     for j in range(tiles):
         store_b(j).start()
-    group_step(3)
-    for j in range(tiles):
-        store_g(j).start()
 
     @pl.when(is_air)
     def _():
@@ -603,6 +667,7 @@
     _, levels, columns = state.shape
     tiles = columns // LANES
     padded = tiles + 2 * RIM // LANES
+    ringed = tiles + 2 * RING
     pairs, block = pair_rows.shape[1:]
     pieces = block // (2 * LANES)
     bulk = levels - SUB
@@ -611,8 +676,10 @@
     dma = pltpu.SemaphoreType.DMA
     scratch = (
         [pltpu.VMEM((padded, bulk, LANES), F32)] * STEPS
-        + [pltpu.VMEM((padded, SUB, LANES), F32)] * STEPS
+        + [pltpu.VMEM((tiles + 2 * REACH, SUB, LANES), F32)] * STEPS
         + [pltpu.VMEM((tiles, bulk, LANES), F32), pltpu.VMEM((tiles, SUB, LANES), F32)]
+        + [pltpu.VMEM((ringed, SUB, LANES), jnp.int32), pltpu.VMEM((ringed, SUB, LANES), F32)]
+        + [pltpu.VMEM((ringed * EDGES, LANES), jnp.int32), pltpu.SMEM((ringed * EDGES, LANES), jnp.int32)]
         + [
             pltpu.VMEM(pair_cols.shape, jnp.int32),
             pltpu.VMEM((pairs, block, block), F32),
@@ -627,7 +694,7 @@
             pltpu.VMEM((tiles, SUB, LANES), F32),
             pltpu.VMEM((tiles, SUB, LANES), F32),
             pltpu.VMEM((nc - 1, tiles, SUB, LANES), F32),
-            pltpu.VMEM((tiles, SUB, LANES), F32),
+            pltpu.VMEM((ringed, SUB, LANES), F32),
         ]
         + [pltpu.VMEM((nd + EDGES * tiles, LANES), jnp.int32), pltpu.SMEM((nd + EDGES * tiles, LANES), jnp.int32)]
         + [pltpu.VMEM((SUB, LANES), F32)] * 2 + [pltpu.VMEM((nc, SUB, LANES), F32), dma, dma((2,)), dma((2,))]

time: 48.5 us -> 46.8 us (0.965)
  Pallas kernels: 45.9 us -> 44.2 us
    pallas_call x1, Pallas kernels: 43.9 us -> 42.2 us  [windowed(): pl.pallas_call(functools.partial(interval_kernel, nd, nc, tiles, levels,...]
where the time goes in v7:
time: 46.8 us; the launch traced here: 46.5 us
  Pallas kernels  44.2 us (94%)
  local copies, waits for them, and re-layouts  1.2 us (3%)
  between operations  0.88 us (2%)
    pallas_call x1, Pallas kernels, windowed(): pl.pallas_call(functools.partial(interval_kernel, nd, nc, tiles, levels,...  42.2 us
    pallas_call x1, Pallas kernels, publish(): pl.pallas_call(functools.partial(publish_kernel, parts), out_shape=jax.Sh...  1.98 us
    slice x1, local copies, waits for them, and re-layouts, local(): done = lax.while_loop(lambda c: c[0], anyway, (flags[0, 0] > 0, fast))  1.19 us

profile of v7, /device:TPU:0, one launch (start us, length us, event | category | flops | bytes accessed | tf_op | source)
XLA Modules:
  0.0 46.5 jit_solution(11273521639262878117)
XLA Ops:
  0.0 0.0 copy-start.1
  0.0 0.0 copy-start.2
  0.0 0.0 copy-start.4
  0.0 42.2 %interval.1 = (f32[128,2048]{1,0:T(8,128)}, f32[8,128]{1,0:T(8,128)}) custom-call(s32[4,2048]{1,0:T(4,128)} %bitcast.130, f32[4,2048]{1,0:T(4,128)} %bitcast.133, s32[1,2048]{1,0:T(1,128)} %bitcast.151, s32[16,512]{1,0:T(8,128)} %bitcast.37.rows, s32[16,32]{1,0:T(8,128)} %bitcast.149, f32[128,2048]{1,0:T(8,128)} %bitcast.39.state_hbm, ...), custom_call_target="tpu_custom_call" | custom-call | flops 1000000000 | bytes 100000000 | tf_op jit(solution)/shard_map/interval/pallas_call | solution.py:705
  42.2 1.2 %slice.114 = f32[1,1]{1,0:T(1,128)} slice(f32[8,128]{1,0:T(8,128)} %get-tuple-element.169), slice={[0:1], [0:1]} | slice | bytes 8 | tf_op jit(solution)/shard_map/slice | solution.py:757
  44.1 0.0 copy-done.1
  44.1 0.0 copy-done.2
  44.1 0.0 copy-done.4
  44.1 0.2 while.23
  44.4 2.0 %publish.1 = f32[128,2048]{1,0:T(8,128)} custom-call(f32[128,2048]{1,0:T(8,128)} %get-tuple-element.386), custom_call_target="tpu_custom_call" | custom-call | tf_op jit(solution)/shard_map/publish/pallas_call | solution.py:739
Async XLA Ops:
  0.0 44.1 %copy-start.1 = (s32[1,4,2048]{2,1,0:T(4,128)S(1)}, s32[1,4,2048]{2,1,0:T(4,128)}, u32[]{:S(2)}) copy-start(s32[1,4,2048]{2,1,0:T(4,128)} %param.15) | copy-start | bytes 98308
  0.0 44.1 %copy-start.2 = (f32[1,4,2048]{2,1,0:T(4,128)S(1)}, f32[1,4,2048]{2,1,0:T(4,128)}, u32[]{:S(2)}) copy-start(f32[1,4,2048]{2,1,0:T(4,128)} %param.16) | copy-start | bytes 98308
  0.0 44.1 %copy-start.4 = (s32[32,16]{0,1:T(8,128)S(1)}, s32[32,16]{0,1:T(8,128)}, u32[]{:S(2)}) copy-start(s32[32,16]{0,1:T(8,128)} %param.18) | copy-start | bytes 6148

commit v8 on v7

--- a/solution.py
+++ b/solution.py
@@ -103,7 +103,7 @@
 def interval_kernel(nd, nc, tiles, levels, block, pairs,
                     nbr, coef, mask, rows, sources, state_hbm, cols_hbm, w_hbm,
                     out, flag_out,
-                    pb0, pb1, pb2, pb3, gx0, gx1, gx2, gx3, outb, outg, ix, cx, tabw, tab2,
+                    pb0, pb1, pb2, pb3, gx0, gx1, gx2, gx3, outb, outg, ix, cx, tabw, tab2, blocksum,
                     cols, wbuf, compact, slots, gsl, zslots, usl, nslots, gnear, unear, sea, fpart, fgot, force,
                     tabv, tab, flag, pflag, flags_in, tab_sem, gsend, grecv,
                     load_sem, w_sem, cols_sem, out_sem,
@@ -498,14 +498,14 @@
 
     bulk_step(0)
 
-    @pl.when(is_air)
-    def _():
-        arrived(sea, srecv)
-        arrived(flag, grecv.at[0])
-        pltpu.make_async_copy(w_hbm, wbuf, w_sem).wait()
-        flag[...] = jnp.maximum(flag[...], flags_in[ocean])
-        for n in range(NEAR_COUNT + 1):
-            zslots[n, pieces] = flag[...]
+    def air_blocks(part):
+        if part == 0:
+            arrived(sea, srecv)
+            arrived(flag, grecv.at[0])
+            pltpu.make_async_copy(w_hbm, wbuf, w_sem).wait()
+            flag[...] = jnp.maximum(flag[...], flags_in[ocean])
+            for n in range(NEAR_COUNT + 1):
+                zslots[n, pieces] = flag[...]
         sea_table = doubled(sea, 0)
 
         def dense(p, slot):
@@ -547,32 +547,46 @@
                 u_near(n).start()
             return scatter(eight, index)
 
-        arrived(gnear.at[pl.ds(0, NEAR_COUNT - 1)], arecv.at[1])
-        total = near_block(1)
-        total = total + near_block(NEAR_COUNT - 1)
-
-        arrived(gsl.at[pl.ds(0, far_count)], arecv.at[0])
-        src = tab[0, T_ESRC]
-        eight, z, index = dense(tab[0, T_EP], [gsl[src, i] for i in range(pieces)])
-        put(zslots, NEAR_COUNT, z)
-
-        def send(r, _):
-            u_copy(r).start()
-            return 0
-        lax.fori_loop(NEAR + 1, nd - NEAR, send, 0)
-        total = total + scatter(jnp.where(tab[0, T_EVALID] == 1, eight, 0.0), index)
+        if part == 0:
+            arrived(gnear.at[pl.ds(0, NEAR_COUNT - 1)], arecv.at[1])
+            total = near_block(1)
+            total = total + near_block(NEAR_COUNT - 1)
+
+            arrived(gsl.at[pl.ds(0, far_count)], arecv.at[0])
+            src = tab[0, T_ESRC]
+            eight, z, index = dense(tab[0, T_EP], [gsl[src, i] for i in range(pieces)])
+            put(zslots, NEAR_COUNT, z)
+
+            def send(r, _):
+                u_copy(r).start()
+                return 0
+            lax.fori_loop(NEAR + 1, nd - NEAR, send, 0)
+            blocksum[...] = total + scatter(jnp.where(tab[0, T_EVALID] == 1, eight, 0.0), index)
+            return
+        total = blocksum[...]
         for n in range(2, NEAR_COUNT - 1):
             total = total + near_block(n)
         total = total + near_block(0)
         for h in range(tiles):
-            part = total[h * SUB:(h + 1) * SUB]
-            fpart[h] = part + pltpu.roll(part, FIELDS, axis=0)
+            part_h = total[h * SUB:(h + 1) * SUB]
+            fpart[h] = part_h + pltpu.roll(part_h, FIELDS, axis=0)
         pltpu.make_async_remote_copy(
             src_ref=fpart, dst_ref=fgot.at[comp], send_sem=fsend, recv_sem=frecv,
             device_id=(ocean, dom), device_id_type=MESH).start()
 
+    @pl.when(is_air)
+    def _():
+        air_blocks(0)
+
+    bulk_edges(1)
+
+    @pl.when(is_air)
+    def _():
+        air_blocks(1)
+
     ring_windows()
-    bulk_step(1)
+    bulk_inner(1, 0, inner)
+    bulk_edges(2)
 
     @pl.when(is_air)
     def _():
@@ -615,7 +629,8 @@
         for c in range(1, nc):
             plane_flag_copy(c).start()
 
-    bulk_step(2)
+    bulk_inner(2, 0, inner)
+    bulk_edges(3)
     pltpu.make_async_copy(tabw, tab2, tab_sem).wait()
     for c in ring_copies(force, RING, 3):
         c.wait()
@@ -623,7 +638,7 @@
         ring_step(s)
     for j in range(tiles):
         store_g(j).start()
-    bulk_step(3)
+    bulk_inner(3, 0, inner)
 
     for j in range(tiles):
         store_b(j).start()
@@ -680,6 +695,7 @@
         + [pltpu.VMEM((tiles, bulk, LANES), F32), pltpu.VMEM((tiles, SUB, LANES), F32)]
         + [pltpu.VMEM((ringed, SUB, LANES), jnp.int32), pltpu.VMEM((ringed, SUB, LANES), F32)]
         + [pltpu.VMEM((ringed * EDGES, LANES), jnp.int32), pltpu.SMEM((ringed * EDGES, LANES), jnp.int32)]
+        + [pltpu.VMEM((tiles * SUB, LANES), F32)]
         + [
             pltpu.VMEM(pair_cols.shape, jnp.int32),
             pltpu.VMEM((pairs, block, block), F32),

time: 46.8 us -> 48.8 us (1.043)
  Pallas kernels: 44.2 us -> 46.2 us
    pallas_call x1, Pallas kernels: 42.2 us -> 44.2 us  [windowed(): pl.pallas_call(functools.partial(interval_kernel, nd, nc, tiles, levels,...]
where the time goes in v8:
time: 48.8 us; the launch traced here: 48.5 us
  Pallas kernels  46.2 us (95%)
  local copies, waits for them, and re-layouts  1.2 us (2%)
  between operations  0.88 us (2%)
    pallas_call x1, Pallas kernels, windowed(): pl.pallas_call(functools.partial(interval_kernel, nd, nc, tiles, levels,...  44.2 us
    pallas_call x1, Pallas kernels, publish(): pl.pallas_call(functools.partial(publish_kernel, parts), out_shape=jax.Sh...  1.98 us
    slice x1, local copies, waits for them, and re-layouts, local(): done = lax.while_loop(lambda c: c[0], anyway, (flags[0, 0] > 0, fast))  1.19 us

profile of v8, /device:TPU:0, one launch (start us, length us, event | category | flops | bytes accessed | tf_op | source)
XLA Modules:
  0.0 48.5 jit_solution(11460165040535856404)
XLA Ops:
  0.0 0.0 copy-start.1
  0.0 0.0 copy-start.2
  0.0 0.0 copy-start.4
  0.0 44.2 %interval.1 = (f32[128,2048]{1,0:T(8,128)}, f32[8,128]{1,0:T(8,128)}) custom-call(s32[4,2048]{1,0:T(4,128)} %bitcast.130, f32[4,2048]{1,0:T(4,128)} %bitcast.133, s32[1,2048]{1,0:T(1,128)} %bitcast.151, s32[16,512]{1,0:T(8,128)} %bitcast.37.rows, s32[16,32]{1,0:T(8,128)} %bitcast.149, f32[128,2048]{1,0:T(8,128)} %bitcast.39.state_hbm, ...), custom_call_target="tpu_custom_call" | custom-call | flops 1000000000 | bytes 100000000 | tf_op jit(solution)/shard_map/interval/pallas_call | solution.py:721
  44.2 1.2 %slice.114 = f32[1,1]{1,0:T(1,128)} slice(f32[8,128]{1,0:T(8,128)} %get-tuple-element.169), slice={[0:1], [0:1]} | slice | bytes 8 | tf_op jit(solution)/shard_map/slice | solution.py:773
  46.1 0.0 copy-done.1
  46.1 0.0 copy-done.2
  46.1 0.0 copy-done.4
  46.1 0.2 while.23
  46.4 2.0 %publish.1 = f32[128,2048]{1,0:T(8,128)} custom-call(f32[128,2048]{1,0:T(8,128)} %get-tuple-element.386), custom_call_target="tpu_custom_call" | custom-call | tf_op jit(solution)/shard_map/publish/pallas_call | solution.py:755
Async XLA Ops:
  0.0 46.1 %copy-start.1 = (s32[1,4,2048]{2,1,0:T(4,128)S(1)}, s32[1,4,2048]{2,1,0:T(4,128)}, u32[]{:S(2)}) copy-start(s32[1,4,2048]{2,1,0:T(4,128)} %param.15) | copy-start | bytes 98308
  0.0 46.1 %copy-start.2 = (f32[1,4,2048]{2,1,0:T(4,128)S(1)}, f32[1,4,2048]{2,1,0:T(4,128)}, u32[]{:S(2)}) copy-start(f32[1,4,2048]{2,1,0:T(4,128)} %param.16) | copy-start | bytes 98308
  0.0 46.1 %copy-start.4 = (s32[32,16]{0,1:T(8,128)S(1)}, s32[32,16]{0,1:T(8,128)}, u32[]{:S(2)}) copy-start(s32[32,16]{0,1:T(8,128)} %param.18) | copy-start | bytes 6148

commit v9 on v7

--- a/solution.py
+++ b/solution.py
@@ -504,8 +504,7 @@
         arrived(flag, grecv.at[0])
         pltpu.make_async_copy(w_hbm, wbuf, w_sem).wait()
         flag[...] = jnp.maximum(flag[...], flags_in[ocean])
-        for n in range(NEAR_COUNT + 1):
-            zslots[n, pieces] = flag[...]
+        marked = jnp.concatenate([flag[pl.ds(0, FIELDS), :]] * (block // LANES), axis=1) > 0.5
         sea_table = doubled(sea, 0)
 
         def dense(p, slot):
@@ -520,7 +519,7 @@
                  + lax.dot_general(x, wl, dims, preferred_element_type=F32))
             z = jnp.dot(v, wh, preferred_element_type=F32) + jnp.dot(v, wl, preferred_element_type=F32)
             y = y[:FIELDS] + y[FIELDS:]
-            z = z[:FIELDS] + z[FIELDS:]
+            z = jnp.where(marked, jnp.nan, z[:FIELDS] + z[FIELDS:])
             yh = y.astype(BF16).astype(F32)
             return jnp.concatenate([yh, y - yh], axis=0), z, index
 
@@ -574,6 +573,9 @@
     ring_windows()
     bulk_step(1)
 
+    def mark_of(piece):
+        return jnp.where(piece != piece, 1.0, 0.0)
+
     @pl.when(is_air)
     def _():
         arrived(unear.at[pl.ds(0, NEAR_COUNT - 1)], urecv.at[1])
@@ -581,11 +583,11 @@
         plane = flag[...]
         for n, r in enumerate(near_rel):
             if r:
-                plane = jnp.maximum(plane, unear[n, pieces])
+                plane = jnp.maximum(plane, mark_of(unear[n, 0]))
             total = total + scatter(split_rows([unear[n, i] for i in range(pieces)]), cols_of(lax.rem(dom + r, nd)))
         arrived(usl.at[pl.ds(0, far_count)], urecv.at[0])
         for r in range(NEAR + 1, nd - NEAR):
-            plane = jnp.maximum(plane, usl[lax.rem(dom + r, nd), pieces])
+            plane = jnp.maximum(plane, mark_of(usl[lax.rem(dom + r, nd), 0]))
         pflag[...] = plane
         for e in range(EXTRAS):
             t = tab[0, T_EXT + e]
@@ -686,11 +688,11 @@
             pltpu.VMEM((EXTRAS, pieces, SUB, LANES), F32),
             pltpu.VMEM((nd, pieces, SUB, LANES), F32),
             pltpu.VMEM((nd, pieces, SUB, LANES), F32),
-            pltpu.VMEM((NEAR_COUNT + 1, pieces + 1, SUB, LANES), F32),
-            pltpu.VMEM((nd, pieces + 1, SUB, LANES), F32),
+            pltpu.VMEM((NEAR_COUNT + 1, pieces, SUB, LANES), F32),
+            pltpu.VMEM((nd, pieces, SUB, LANES), F32),
             pltpu.VMEM((NEAR_COUNT, pieces, SUB, LANES), F32),
             pltpu.VMEM((NEAR_COUNT, pieces, SUB, LANES), F32),
-            pltpu.VMEM((NEAR_COUNT, pieces + 1, SUB, LANES), F32),
+            pltpu.VMEM((NEAR_COUNT, pieces, SUB, LANES), F32),
             pltpu.VMEM((tiles, SUB, LANES), F32),
             pltpu.VMEM((tiles, SUB, LANES), F32),
             pltpu.VMEM((nc - 1, tiles, SUB, LANES), F32),

time: 46.8 us -> 46.7 us (level)
  no operation moved by 1% of the time
where the time goes in v9:
time: 46.7 us; the launch traced here: 46.4 us
  Pallas kernels  44.1 us (94%)
  local copies, waits for them, and re-layouts  1.2 us (3%)
  between operations  0.88 us (2%)
    pallas_call x1, Pallas kernels, windowed(): pl.pallas_call(functools.partial(interval_kernel, nd, nc, tiles, levels,...  42.1 us
    pallas_call x1, Pallas kernels, publish(): pl.pallas_call(functools.partial(publish_kernel, parts), out_shape=jax.Sh...  1.98 us
    slice x1, local copies, waits for them, and re-layouts, local(): done = lax.while_loop(lambda c: c[0], anyway, (flags[0, 0] > 0, fast))  1.19 us

profile of v9, /device:TPU:0, one launch (start us, length us, event | category | flops | bytes accessed | tf_op | source)
XLA Modules:
  0.0 46.4 jit_solution(6127882735205183112)
XLA Ops:
  0.0 0.0 copy-start.1
  0.0 0.0 copy-start.2
  0.0 0.0 copy-start.4
  0.0 42.1 %interval.1 = (f32[128,2048]{1,0:T(8,128)}, f32[8,128]{1,0:T(8,128)}) custom-call(s32[4,2048]{1,0:T(4,128)} %bitcast.130, f32[4,2048]{1,0:T(4,128)} %bitcast.133, s32[1,2048]{1,0:T(1,128)} %bitcast.151, s32[16,512]{1,0:T(8,128)} %bitcast.37.rows, s32[16,32]{1,0:T(8,128)} %bitcast.149, f32[128,2048]{1,0:T(8,128)} %bitcast.39.state_hbm, ...), custom_call_target="tpu_custom_call" | custom-call | flops 1000000000 | bytes 100000000 | tf_op jit(solution)/shard_map/interval/pallas_call | solution.py:707
  42.1 1.2 %slice.114 = f32[1,1]{1,0:T(1,128)} slice(f32[8,128]{1,0:T(8,128)} %get-tuple-element.169), slice={[0:1], [0:1]} | slice | bytes 8 | tf_op jit(solution)/shard_map/slice | solution.py:759
  44.0 0.0 copy-done.1
  44.0 0.0 copy-done.2
  44.0 0.0 copy-done.4
  44.0 0.2 while.23
  44.2 2.0 %publish.1 = f32[128,2048]{1,0:T(8,128)} custom-call(f32[128,2048]{1,0:T(8,128)} %get-tuple-element.386), custom_call_target="tpu_custom_call" | custom-call | tf_op jit(solution)/shard_map/publish/pallas_call | solution.py:741
Async XLA Ops:
  0.0 44.0 %copy-start.1 = (s32[1,4,2048]{2,1,0:T(4,128)S(1)}, s32[1,4,2048]{2,1,0:T(4,128)}, u32[]{:S(2)}) copy-start(s32[1,4,2048]{2,1,0:T(4,128)} %param.15) | copy-start | bytes 98308
  0.0 44.0 %copy-start.2 = (f32[1,4,2048]{2,1,0:T(4,128)S(1)}, f32[1,4,2048]{2,1,0:T(4,128)}, u32[]{:S(2)}) copy-start(f32[1,4,2048]{2,1,0:T(4,128)} %param.16) | copy-start | bytes 98308
  0.0 44.0 %copy-start.4 = (s32[32,16]{0,1:T(8,128)S(1)}, s32[32,16]{0,1:T(8,128)}, u32[]{:S(2)}) copy-start(s32[32,16]{0,1:T(8,128)} %param.18) | copy-start | bytes 6148

commit v10 on v9

--- a/solution.py
+++ b/solution.py
@@ -753,10 +753,10 @@
     fast, flags = windowed(state, neighbors, edge_coef, sea_mask, pair_rows, pair_cols, remap_weight, sources)
 
     def anyway(_):
-        return False, general(state, neighbors, edge_coef, sea_mask,
+        return jnp.zeros_like(flags), general(state, neighbors, edge_coef, sea_mask,
                               with_layout_constraint(sources, Layout((0, 1))).T, pair_rows, pair_cols, remap_weight)
 
-    done = lax.while_loop(lambda c: c[0], anyway, (flags[0, 0] > 0, fast))
+    done = lax.while_loop(lambda c: c[0][0, 0] > 0, anyway, (flags, fast))
     return publish(done[1])[None]
 
 

time: 46.7 us -> 371 us (7.94)
  other arithmetic: 0 us -> 165 us
  local copies, waits for them, and re-layouts: 1.2 us -> 106 us
  matrix products: 0 us -> 28.8 us
  starting transfers between devices: 0 us -> 20.9 us
  Pallas kernels: 44.1 us -> 48.1 us
    scatter-add x0 -> x4, other arithmetic: none -> 163 us  [the longest x1 111 us: general(): jnp.zeros((fields, column_count), jnp.float32).at[:, my_columns]]
    gather x0 -> x6, local copies, waits for them, and re-layouts: none -> 91.6 us  [the longest x2 59.6 us: general(): air_values = surface[:, my_columns] * partner[None, :, None]]
    dot_general x0 -> x2, matrix products: none -> 28.8 us  [the longest x1 17.3 us: general(): jnp.einsum('qbj,fqj->fqb', weights_here, incoming, precision=highest)]
    all_to_all x0 -> x2, starting transfers between devices: none -> 20.9 us  [the longest x1 11.1 us: general(): lax.all_to_all(to_sea, ('comp', 'dom'), split_axis=1, concat_axis=1, tile...]
    mul x0 -> x3, local copies, waits for them, and re-layouts: none -> 7.87 us  [the longest x1 5.06 us: general(): arrived = got_air[:, slot_index] * partner[None, :, None]]
    pallas_call x1, Pallas kernels: 42.1 us -> 46.1 us  [windowed(): pl.pallas_call(functools.partial(interval_kernel, nd, nc, tiles, levels,...]
  transfers between devices with their start and end apart: 0 -> 2, of which waited for: 0 -> 0; matrix products, arithmetic and copies ran while one was open for 0% -> 18% of each run, Pallas kernels for 0% -> 12%
where the time goes in v10:
time: 371 us; the launch traced here: 370 us
  other arithmetic  165 us (44%)
  local copies, waits for them, and re-layouts  106 us (29%)
  Pallas kernels  48.1 us (13%)
  matrix products  28.8 us (8%)
  starting transfers between devices  20.9 us (6%)
    scatter-add x1, other arithmetic, general(): jnp.zeros((fields, column_count), jnp.float32).at[:, my_columns]  111 us
    gather x2, local copies, waits for them, and re-layouts, general(): air_values = surface[:, my_columns] * partner[None, :, None]  59.6 us
    pallas_call x1, Pallas kernels, windowed(): pl.pallas_call(functools.partial(interval_kernel, nd, nc, tiles, levels,...  46.1 us
    scatter-add x1, other arithmetic, general(): jnp.zeros((fields, column_count), jnp.float32).at[:, rows_here]  45.4 us
    gather x2, local copies, waits for them, and re-layouts, general(): sea_values = surface[:, rows_here]  30.6 us
    dot_general x1, matrix products, general(): jnp.einsum('qbj,fqj->fqb', weights_here, incoming, precision=highest)  17.3 us
    dot_general x1, matrix products, general(): jnp.einsum('qbj,fqb->fqj', weights_here, sea_values, precision=highest)  11.5 us
    all_to_all x1, starting transfers between devices, general(): lax.all_to_all(to_sea, ('comp', 'dom'), split_axis=1, concat_axis=1, tile...  11.1 us
  transfers between devices with their start and end apart: 2, of which 0 were waited for; matrix products, arithmetic and copies ran while one was open for 18% of the time, Pallas kernels for 12%

profile of v10, /device:TPU:0, one launch (start us, length us, event | category | flops | bytes accessed | tf_op | source)
XLA Modules:
  0.0 369.9 jit_solution(16049587431094613764)
XLA Ops:
  0.0 0.7 fusion.20
  0.7 0.1 copy.26
  0.8 1.5 select_reduce_fusion
  2.4 0.8 slice_bitcast_fusion
  3.2 0.4 copy.27
  3.6 54.4 %gather_fusion.4 = f32[16384,4]{1,0:T(8,128)} fusion(f32[4,2048]{0,1:T(8,128)S(1)} %copy.27, s32[16384]{0:T(1024)S(1)} %broadcast_clamp_fusion.4), kind=kCustom, calls=%fused_computation.4 | custom fusion | bytes 589824 | tf_op jit(solution)/shard_map/while/body/gather | solution.py:72
  58.0 5.2 %copy.35 = f32[32,512,4]{1,0,2:T(8,128)S(1)} copy(f32[32,512,4]{2,1,0:T(8,128)} %bitcast.143) | data formatting | bytes 524288 | tf_op jit(solution)/shard_map/while/body/gather | solution.py:72
  63.3 0.1 multiply_bitcast_fusion
  63.4 0.2 copy.29
  63.5 1.1 broadcast.300.clone
  64.6 4.2 %scatter_fusion = f32[4,128,512]{2,0,1:T(4,128)} fusion(f32[4,128,512]{2,0,1:T(4,128)} %broadcast.300.clone, s32[32]{0:T(128)S(1)} %fusion.17, f32[32,4,512]{2,1,0:T(4,128)S(1)} %copy.29), kind=kCustom, calls=%fused_computation.8 | custom fusion | flops 65536 | bytes 786560 | tf_op jit(solution)/shard_map/while/body/scatter-add | solution.py:73
  68.9 11.1 %all-to-all-start = ((f32[4,128,512]{2,0,1:T(4,128)}), f32[4,128,512]{2,0,1:T(4,128)S(1)}, u32[]{:S(2)}, u32[]{:S(2)}) async-start(f32[4,128,512]{2,0,1:T(4,128)} %scatter_fusion), calls=%async_computation | async-start | bytes 2097152 | tf_op jit(solution)/shard_map/while/body/all_to_all | solution.py:75
  80.1 1.3 copy.34
  81.4 27.8 %gather_fusion.6 = f32[8192,4]{1,0:T(8,128)} fusion(f32[4,2048]{0,1:T(8,128)S(1)} %copy.27, s32[8192]{0:T(1024)S(1)} %broadcast_clamp_fusion.5), kind=kCustom, calls=%fused_computation.6 | custom fusion | bytes 294912 | tf_op jit(solution)/shard_map/while/body/gather | solution.py:68
  109.2 2.8 copy.32
  112.0 0.2 fusion.16
  112.2 11.5 %convolution_multiply_fusion = f32[16,4,512]{2,1,0:T(4,128)S(1)} fusion(f32[16,512,4]{1,2,0:T(4,128)S(1)} %copy.32, f32[]{:T(128)S(6)} %select_n.176, f32[1,16,512,512]{3,2,1,0:T(8,128)} %param.21), kind=kOutput, calls=%fused_computation.39 | convolution fusion | flops 201359360 | bytes 17039364 | tf_op jit(solution)/shard_map/while/body/qbj,fqb->fqj/dot_general | solution.py:69
  123.8 1.2 broadcast.300.clone.1
  125.0 2.4 scatter_fusion.1
  127.4 9.8 %all-to-all-start.1 = ((f32[4,128,512]{2,0,1:T(4,128)}), f32[4,128,512]{2,0,1:T(4,128)S(1)}, u32[]{:S(2)}, u32[]{:S(2)}) async-start(f32[4,128,512]{2,0,1:T(4,128)} %scatter_fusion.1), calls=%async_computation.1 | async-start | bytes 2097152 | tf_op jit(solution)/shard_map/while/body/all_to_all | solution.py:76
  137.2 46.1 %interval.1 = (f32[128,2048]{1,0:T(8,128)}, f32[8,128]{1,0:T(8,128)}) custom-call(s32[4,2048]{1,0:T(4,128)S(1)} %bitcast.129, f32[4,2048]{1,0:T(4,128)S(1)} %bitcast.132, s32[1,2048]{1,0:T(1,128)S(1)} %bitcast.148, s32[16,512]{1,0:T(8,128)} %bitcast.151, s32[16,32]{1,0:T(8,128)} %bitcast.155, f32[128,2048]{1,0:T(8,128)} %bitcast.145, ...), custom_call_target="tpu_custom_call" | custom-call | flops 1000000000 | bytes 100000000 | tf_op jit(solution)/shard_map/interval/pallas_call | solution.py:707
  183.3 0.6 gather_fusion.5
  183.9 17.3 %convolution_multiply_fusion.1 = f32[16,4,512]{2,1,0:T(4,128)S(1)} fusion(f32[16,4,512]{2,1,0:T(4,128)S(1)} %gather_fusion.5, f32[]{:T(128)S(6)} %select_n.176, f32[1,16,512,512]{3,2,1,0:T(8,128)} %param.21), kind=kOutput, calls=%fused_computation.40 | convolution fusion | flops 201359360 | bytes 17039364 | tf_op jit(solution)/shard_map/while/body/qbj,fqj->fqb/dot_general | solution.py:79
  201.2 2.6 copy.30
  203.8 0.7 gather_fusion.7
  204.5 0.1 broadcast_multiply_fusion
  204.6 5.1 %copy.33 = f32[16384,4]{1,0:T(8,128)} copy(f32[16384,4]{0,1:T(4,128)S(1)} %bitcast.146) | data formatting | bytes 524288 | tf_op jit(solution)/shard_map/while/body/mul | solution.py:81
  209.7 45.4 %scatter_custom_fusion.1 = f32[4,2048]{0,1:T(8,128)} fusion(s32[8192]{0:T(1024)S(1)} %bitcast.153, f32[8192,4]{1,0:T(8,128)} %copy.30, f32[]{:T(128)} %constant.193.clone.1), kind=kCustom, calls=%fused_computation.44 | custom fusion | flops 32768 | bytes 33280 | tf_op jit(solution)/shard_map/while/body/scatter-add | solution.py:80
  255.1 110.6 %scatter_custom_fusion.3 = f32[4,2048]{0,1:T(8,128)} fusion(s32[16384]{0:T(1024)S(1)} %bitcast.150, f32[16384,4]{1,0:T(8,128)} %copy.33, f32[]{:T(128)} %constant.193.clone.1), kind=kCustom, calls=%fused_computation.42 | custom fusion | flops 65536 | bytes 33280 | tf_op jit(solution)/shard_map/while/body/scatter-add | solution.py:82
  365.6 2.1 while.40
  365.6 1.2 slice.168
  367.7 2.0 publish.1
  (28 shorter events, 0.1 us)
Async XLA Ops:
  0.0 64.6 %copy-start.7 = (s32[32]{0:T(128)}, s32[32]{0:T(128)S(1)}, u32[]{:S(2)}) copy-start(s32[32]{0:T(128)S(1)} %fusion.17) | copy-start | bytes 388
  63.2 16.8 %copy-start.5 = (s32[1,16,512]{2,1,0:T(8,128)S(1)}, s32[1,16,512]{2,1,0:T(8,128)}, u32[]{:S(2)}) copy-start(s32[1,16,512]{2,1,0:T(8,128)} %param.19) | copy-start | bytes 98308
  63.2 16.8 %copy-start.3 = (f32[1,128,2048]{2,1,0:T(8,128)S(1)}, f32[1,128,2048]{2,1,0:T(8,128)}, u32[]{:S(2)}) copy-start(f32[1,128,2048]{2,1,0:T(8,128)} %param.14) | copy-start | bytes 3145732
  68.9 58.5 %all-to-all-start = ((f32[4,128,512]{2,0,1:T(4,128)}), f32[4,128,512]{2,0,1:T(4,128)S(1)}, u32[]{:S(2)}, u32[]{:S(2)}) async-start(f32[4,128,512]{2,0,1:T(4,128)} %scatter_fusion), calls=%async_computation | async-start | bytes 2097152 | tf_op jit(solution)/shard_map/while/body/all_to_all | solution.py:75
  80.1 32.0 %copy-start.6 = (s32[32,16]{0,1:T(8,128)S(1)}, s32[32,16]{0,1:T(8,128)}, u32[]{:S(2)}) copy-start(s32[32,16]{0,1:T(8,128)} %param.18) | copy-start | bytes 6148
  112.2 24.9 %copy-start.1 = (s32[1,4,2048]{2,1,0:T(4,128)S(1)}, s32[1,4,2048]{2,1,0:T(4,128)}, u32[]{:S(2)}) copy-start(s32[1,4,2048]{2,1,0:T(4,128)} %param.15) | copy-start | bytes 98308
  112.2 24.9 %copy-start.2 = (f32[1,4,2048]{2,1,0:T(4,128)S(1)}, f32[1,4,2048]{2,1,0:T(4,128)}, u32[]{:S(2)}) copy-start(f32[1,4,2048]{2,1,0:T(4,128)} %param.16) | copy-start | bytes 98308
  112.2 24.9 %copy-start.4 = (s32[2048]{0:T(1024)S(1)}, s32[2048]{0:T(1024)}, u32[]{:S(2)}) copy-start(s32[2048]{0:T(1024)} %param.17) | copy-start | bytes 24580
  127.4 76.5 %all-to-all-start.1 = ((f32[4,128,512]{2,0,1:T(4,128)}), f32[4,128,512]{2,0,1:T(4,128)S(1)}, u32[]{:S(2)}, u32[]{:S(2)}) async-start(f32[4,128,512]{2,0,1:T(4,128)} %scatter_fusion.1), calls=%async_computation.1 | async-start | bytes 2097152 | tf_op jit(solution)/shard_map/while/body/all_to_all | solution.py:76
  137.2 46.1 %copy-start.8 = (s32[32]{0:T(128)S(1)}, s32[32]{0:T(128)}, u32[]{:S(2)}) copy-start(s32[32]{0:T(128)} %copy-done.7) | copy-start | bytes 388
